TPU v7x, 128 devices: a whole 4x4x4 slice. The times are simulated.
128 devices in a mesh: gx: 8 (over x, core), gy: 8 (over y, z_lo), ga: 2 (over z_hi).
Axes of the slice: x: 4, y: 4, z: 4 (z_hi: 2, z_lo: 2; z = z_hi * 2 + z_lo), core: 2. Of those that a mesh axis runs over, the one named last changes fastest.
Arguments:
- level_set: float32 [256, 256, 512], P('gx', 'gy', 'ga'), may hold values from -2 to 2
- displacement_prev: float32 [3, 256, 256, 512], P(None, 'gx', 'gy', 'ga'), may hold values from -6 to 6
- traction: float32 [3], replicated, may hold values from -3 to 3
- load_mask: int32 [256, 256, 512], P('gx', 'gy', 'ga'), may hold values 0 or 1
- support_mask: int32 [256, 256, 512], P('gx', 'gy', 'ga'), may hold values 0 or 1
- extension: bfloat16 [256, 256], P('gy'), as said below
- tile_count: int32 [8, 16], replicated, may hold values from 1 to 8, 64 in all within a row
- tile_list: int32 [128, 8], P(('gx', 'gy', 'ga')), may hold values from 0 to 7, each once within a row
Outputs:
- displacement: float32 [3, 256, 256, 512], P(None, 'gx', 'gy', 'ga')
- level_set_new: float32 [256, 256, 512], P('gx', 'gy', 'ga')
Inputs may be any that keep to these rules, and one draw needn't show every extreme that they name: Each row of tile_count sums to 64. Each row of tile_list is a permutation; only the first tile_count entries of a device's row are read. extension is symmetric.
All inputs are finite; a program needn't handle non-finite values. No bound on the sum of `load_mask` or of `support_mask` on one device may be relied on, other than what follows from the above.
Results may differ from a plain program's by a relative error of at most 0.0014.
Values may be sent and summed in bfloat16 or wider, within the bound.
No kernel may reach another device: no remote copies, remote signals or barrier semaphores. Data moves between devices by JAX's collectives and lax.ppermute only.
A program may use at most 256 MiB of HBM per device.

v0:
```python
import jax
import jax.numpy as jnp
from jax import lax
from jax.sharding import PartitionSpec as P

TILE = 32
JACOBI = 3
SWEEPS = 4


emin = 0.05
coupling = 0.5
relax = 0.6
advance_step = 0.5
pseudo_step = 0.3


def padded(x, sides, width):
    edges = {}
    for axis, dim in sides:
        peers, length = (lax.axis_size(axis), x.shape[dim])
        up = [(i, (i + 1) % peers) for i in range(peers - 1)]
        last = lax.slice_in_dim(x, length - width, length, axis=dim)
        leading = lax.slice_in_dim(x, 0, width, axis=dim)
        edges[dim] = (
            lax.ppermute(last, axis, up),
            lax.ppermute(leading, axis, [(b, a) for a, b in up]),
        )
    done = []
    for _, dim in sides:
        low, high = edges[dim]
        around = [(width, width) if d in done else (0, 0) for d in range(x.ndim)]
        x = jnp.concatenate([jnp.pad(low, around), x, jnp.pad(high, around)], axis=dim)
        done.append(dim)
    return x


def stiffness(level_values):
    return emin + (1.0 - emin) * 0.5 * (1.0 + jnp.tanh(level_values))


def face_weights(padded_e):
    centre = padded_e[1:-1, 1:-1, 1:-1]
    beside = [
        padded_e[:-2, 1:-1, 1:-1],
        padded_e[2:, 1:-1, 1:-1],
        padded_e[1:-1, :-2, 1:-1],
        padded_e[1:-1, 2:, 1:-1],
        padded_e[1:-1, 1:-1, :-2],
        padded_e[1:-1, 1:-1, 2:],
    ]
    return [0.5 * (centre + neighbour) for neighbour in beside]


def operate(padded_u, weights, centre_e):
    inner = padded_u[:, 1:-1, 1:-1, 1:-1]
    beside = [
        padded_u[:, :-2, 1:-1, 1:-1],
        padded_u[:, 2:, 1:-1, 1:-1],
        padded_u[:, 1:-1, :-2, 1:-1],
        padded_u[:, 1:-1, 2:, 1:-1],
        padded_u[:, 1:-1, 1:-1, :-2],
        padded_u[:, 1:-1, 1:-1, 2:],
    ]
    result = coupling * centre_e[None] * jnp.sum(inner, axis=0, keepdims=True)
    for weight, neighbour in zip(weights, beside):
        result = result + weight[None] * (inner - neighbour)
    return result


def godunov(values, earlier, further):
    growing = jnp.zeros_like(values)
    shrinking = jnp.zeros_like(values)
    for below, above in zip(earlier, further):
        behind_step = values - below
        ahead_step = above - values
        growing = growing + jnp.maximum(
            jnp.square(jnp.maximum(behind_step, 0.0)), jnp.square(jnp.minimum(ahead_step, 0.0))
        )
        shrinking = shrinking + jnp.maximum(
            jnp.square(jnp.minimum(behind_step, 0.0)), jnp.square(jnp.maximum(ahead_step, 0.0))
        )
    return (growing, shrinking)


def reinit_flat(start_values, tile_edge):
    sign_field = start_values / jnp.sqrt(start_values * start_values + 1.0)
    depth_index = jnp.arange(tile_edge * tile_edge) % tile_edge
    first_cell = depth_index == 0
    last_cell = depth_index == tile_edge - 1
    values = start_values
    for repeat in range(SWEEPS):
        x_below = jnp.concatenate([values[:, :1], values[:, :-1]], 1)
        x_above = jnp.concatenate([values[:, 1:], values[:, -1:]], 1)
        y_below = jnp.concatenate([values[:, :, :tile_edge], values[:, :, :-tile_edge]], 2)
        y_above = jnp.concatenate([values[:, :, tile_edge:], values[:, :, -tile_edge:]], 2)
        z_below = jnp.where(
            first_cell, values, jnp.concatenate([values[:, :, :1], values[:, :, :-1]], 2)
        )
        z_above = jnp.where(
            last_cell, values, jnp.concatenate([values[:, :, 1:], values[:, :, -1:]], 2)
        )
        growing, shrinking = godunov(
            values, [x_below, y_below, z_below], [x_above, y_above, z_above]
        )
        values = values - pseudo_step * sign_field * (
            jnp.sqrt(jnp.where(sign_field > 0.0, growing, shrinking)) - 1.0
        )
    return values


def into_tiles(values, tile_edge):
    extent_x, extent_y, extent_z = values.shape
    split = values.reshape(
        extent_x // tile_edge,
        tile_edge,
        extent_y // tile_edge,
        tile_edge,
        extent_z // tile_edge,
        tile_edge,
    )
    return split.transpose(0, 2, 4, 1, 3, 5).reshape(-1, tile_edge, tile_edge * tile_edge)


def from_tiles(tiles, block_shape, tile_edge):
    extent_x, extent_y, extent_z = block_shape
    split = tiles.reshape(
        extent_x // tile_edge,
        extent_y // tile_edge,
        extent_z // tile_edge,
        tile_edge,
        tile_edge,
        tile_edge,
    )
    return split.transpose(0, 3, 1, 4, 2, 5).reshape(block_shape)


def local(
    level_set,
    displacement_prev,
    traction,
    load_mask,
    support_mask,
    extension,
    tile_count,
    tile_list,
):
    padded_phi = padded(
        level_set.astype(jnp.bfloat16), (("gx", 0), ("gy", 1), ("ga", 2)), 1
    ).astype(level_set.dtype)
    padded_e = stiffness(padded_phi)
    centre_e = padded_e[1:-1, 1:-1, 1:-1]
    weights = face_weights(padded_e)
    diagonal = weights[0]
    for weight in weights[1:]:
        diagonal = diagonal + weight
    diagonal = diagonal + coupling * centre_e
    free_cells = (1 - support_mask).astype(jnp.float32)
    force = traction[:, None, None, None] * load_mask.astype(jnp.float32)[None]

    def apply_operator(moving_field):
        padded_u = padded(moving_field, (("gx", 1), ("gy", 2), ("ga", 3)), 1)
        return operate(padded_u, weights, centre_e)

    moving = displacement_prev * free_cells[None]
    for repeat in range(JACOBI):
        image = apply_operator(moving)
        moving = (moving + relax * (force - image) / diagonal[None]) * free_cells[None]
    image = apply_operator(moving)
    energy = jnp.sum(moving * image, axis=0)
    slope = 0.5 * (1.0 - jnp.square(jnp.tanh(level_set)))
    sensitivity = (slope * energy).astype(jnp.bfloat16)
    velocity = jnp.einsum(
        "yk,xkz->xyz",
        extension,
        lax.all_gather(sensitivity, "gy", axis=1, tiled=True),
        preferred_element_type=jnp.float32,
    )
    speed = velocity / (1.0 + jnp.abs(velocity))
    earlier = [
        padded_phi[:-2, 1:-1, 1:-1],
        padded_phi[1:-1, :-2, 1:-1],
        padded_phi[1:-1, 1:-1, :-2],
    ]
    further = [padded_phi[2:, 1:-1, 1:-1], padded_phi[1:-1, 2:, 1:-1], padded_phi[1:-1, 1:-1, 2:]]
    growing, shrinking = godunov(level_set, earlier, further)
    advanced = level_set - advance_step * (
        jnp.maximum(speed, 0.0) * jnp.sqrt(growing) + jnp.minimum(speed, 0.0) * jnp.sqrt(shrinking)
    )
    tiles = into_tiles(advanced, TILE)
    tile_total = tile_list.shape[1]
    group = lax.axis_size("gy") * lax.axis_size("ga")
    source = lax.axis_index("gy") * lax.axis_size("ga") + lax.axis_index("ga")
    counts = lax.dynamic_index_in_dim(tile_count, lax.axis_index("gx"), 0, keepdims=False)
    offsets = jnp.cumsum(counts) - counts
    members = jnp.arange(group)
    own_count = jnp.sum(jnp.where(members == source, counts, 0))
    own_offset = jnp.sum(jnp.where(members == source, offsets, 0))
    entries = jnp.arange(tile_total)
    chosen = (tile_list[0][:, None] == entries[None, :]) & (entries[:, None] < own_count)
    listed = jnp.any(chosen, axis=0)
    per_peer = -(-tile_total // group)
    owners = (own_offset + entries) % group
    column = owners * per_peer + entries // group
    slots = jnp.arange(group * per_peer)
    picker = jnp.sum(
        (chosen[:, :, None] & (column[:, None, None] == slots[None, None, :])).astype(jnp.float32),
        axis=0,
    )
    tile_rows = tiles.reshape(tile_total, -1)
    outgoing = jnp.einsum("tm,tc->mc", picker, tile_rows, precision=lax.Precision.HIGHEST)
    outgoing = outgoing.reshape(group, per_peer, TILE, TILE * TILE)
    received = lax.all_to_all(outgoing, ("gy", "ga"), split_axis=0, concat_axis=0, tiled=True)
    within = jnp.arange(per_peer)[None, :]
    position = (source - offsets[:, None]) % group + within * group
    usable = position < counts[:, None]
    owner_slot = (offsets[:, None] + position) // group
    places = jnp.arange(tile_total // 2)
    selector = ((owner_slot[None] == places[:, None, None]) & usable[None]).astype(jnp.float32)
    selector = selector.reshape(tile_total // 2, group * per_peer)
    owned_tiles = jnp.dot(
        selector, received.reshape(group * per_peer, -1), precision=lax.Precision.HIGHEST
    )
    finished = reinit_flat(owned_tiles.reshape(tile_total // 2, TILE, TILE * TILE), TILE)
    returning = jnp.einsum(
        "qm,qc->mc",
        selector,
        finished.reshape(tile_total // 2, -1),
        precision=lax.Precision.HIGHEST,
    )
    returning = returning.reshape(group, per_peer, TILE, TILE * TILE)
    returned = lax.all_to_all(returning, ("gy", "ga"), split_axis=0, concat_axis=0, tiled=True)
    updated = jnp.dot(
        picker, returned.reshape(group * per_peer, -1), precision=lax.Precision.HIGHEST
    )
    updated = updated.reshape(tiles.shape)
    result_tiles = jnp.where(listed[:, None, None], updated, tiles)
    level_set_new = from_tiles(result_tiles, level_set.shape, TILE)
    return (moving, level_set_new)


def solution(mesh):
    return jax.shard_map(
        local,
        mesh=mesh,
        in_specs=(
            P("gx", "gy", "ga"),
            P(None, "gx", "gy", "ga"),
            P(),
            P("gx", "gy", "ga"),
            P("gx", "gy", "ga"),
            P("gy", None),
            P(),
            P(("gx", "gy", "ga"), None),
        ),
        out_specs=(P(None, "gx", "gy", "ga"), P("gx", "gy", "ga")),
        check_vma=False,
    )
```

profile of v0, /device:TPU:0, one launch (start us, length us, event | category | flops | bytes accessed | tf_op | source)
XLA Modules:
  0.0 493.3 jit_solution(7715689010447941371)
XLA Ops:
  9.6 6.6 %collective-permute-start = (bf16[32,32,1]{2,1,0:T(8,128)(2,1)}, bf16[32,32,1]{2,1,0:T(8,128)(2,1)}, u32[]{:S(2)}, u32[]{:S(2)}) collective-permute-start(bf16[32,32,1]{2,1,0:T(8,128)(2,1)} %get-tuple-element.98), channel_id=1, source_target_pairs={{0,1},{2,3},{4,5},{6,7},{8,9},{10,11},{12,13},{14,15},{16,17},{18,... | collective-permute-start | bytes 6152 | tf_op jit(solution)/shard_map/ppermute | solution.py:26
  18.1 3.5 collective-permute-start.1
  21.8 1.6 fusion.154
  23.4 2.6 fusion.171
  26.0 2.6 copy.166
  28.7 7.4 %collective-permute-start.10 = (f32[3,32,32,1]{2,1,3,0:T(8,128)}, f32[3,32,32,1]{2,1,3,0:T(8,128)S(1)}, u32[]{:S(2)}, u32[]{:S(2)}) collective-permute-start(f32[3,32,32,1]{2,1,3,0:T(8,128)} %copy.166), channel_id=1, source_target_pairs={{0,1},{2,3},{4,5},{6,7},{8,9},{10,11},{12,13},{14,15},{16,17},{18,... | collective-permute-start | bytes 36872 | tf_op jit(solution)/shard_map/ppermute | solution.py:26
  36.0 2.0 copy.168
  42.2 1.9 collective-permute-start.2
  48.2 2.4 convert_element_type.44
  50.6 2.6 copy.167
  53.2 2.6 copy.169
  55.8 3.2 collective-permute-start.8
  60.3 3.9 collective-permute-start.6
  65.6 4.3 multiply_add_fusion
  69.9 3.7 add_add_fusion
  74.0 13.4 %fusion.152 = (f32[32,32,256]{2,1,0:T(8,128)}, f32[3,32,32,256]{3,2,1,0:T(8,128)S(1)}) fusion(f32[32,32,256]{2,1,0:T(8,128)} %copy-done.12, f32[3,32,32,256]{3,2,1,0:T(8,128)S(1)} %copy-done.5, f32[32,32,256]{2,1,0:T(8,128)} %get-tuple-element.16, f32[3,32,32,1]{3,2,1,0:T(8,128)} %copy.169, f32[3,34,1,256]{3,2,1,0:T(1,128)S(1)} %pad.69, ...), kind=kLoop, calls=%fused_computation.310 | loop fusion | flops 38273024 | bytes 18255884 | tf_op jit(solution)/shard_map/reduce_sum | solution.py:65
  87.4 2.6 fusion.168
  90.2 2.6 copy.176
  92.8 6.7 %collective-permute-start.16 = (f32[3,32,32,1]{2,1,3,0:T(8,128)}, f32[3,32,32,1]{2,1,3,0:T(8,128)}, u32[]{:S(2)}, u32[]{:S(2)}) collective-permute-start(f32[3,32,32,1]{2,1,3,0:T(8,128)} %copy.176), channel_id=1, source_target_pairs={{0,1},{2,3},{4,5},{6,7},{8,9},{10,11},{12,13},{14,15},{16,17},{18,... | collective-permute-start | bytes 36872 | tf_op jit(solution)/shard_map/ppermute | solution.py:26
  99.5 1.6 fusion.170
  101.1 2.6 copy.178
  105.7 4.3 collective-permute-start.14
  111.3 4.3 collective-permute-start.12
  117.0 2.6 multiply_multiply_fusion.2
  119.6 2.6 copy.177
  122.2 2.6 copy.179
  126.1 16.4 %fusion.150 = (f32[32,32,256]{2,1,0:T(8,128)}, f32[3,32,32,256]{3,2,1,0:T(8,128)S(1)}) fusion(f32[32,32,256]{2,1,0:T(8,128)} %copy-done.12, f32[3,32,32,256]{3,2,1,0:T(8,128)} %copy-done.3, f32[32,32,256]{2,1,0:T(8,128)} %get-tuple-element.16, f32[3,32,32,1]{3,2,1,0:T(8,128)} %copy.179, f32[3,34,1,256]{3,2,1,0:T(1,128)S(1)} %pad.73, ...), kind=kLoop, calls=%fused_computation.309 | loop fusion | flops 38273024 | bytes 18255884 | tf_op jit(solution)/shard_map/reduce_sum | solution.py:65
  142.5 2.6 fusion.165
  145.3 2.6 copy.186
  147.9 7.6 %collective-permute-start.22 = (f32[3,32,32,1]{2,1,3,0:T(8,128)}, f32[3,32,32,1]{2,1,3,0:T(8,128)}, u32[]{:S(2)}, u32[]{:S(2)}) collective-permute-start(f32[3,32,32,1]{2,1,3,0:T(8,128)} %copy.186), channel_id=1, source_target_pairs={{0,1},{2,3},{4,5},{6,7},{8,9},{10,11},{12,13},{14,15},{16,17},{18,... | collective-permute-start | bytes 36872 | tf_op jit(solution)/shard_map/ppermute | solution.py:26
  157.1 2.6 copy.188
  161.7 4.6 collective-permute-start.20
  167.6 4.5 collective-permute-start.18
  173.5 2.6 multiply_multiply_fusion.1
  176.0 2.6 copy.187
  178.6 2.6 copy.189
  182.5 16.4 %fusion.148 = (f32[32,32,256]{2,1,0:T(8,128)}, f32[3,32,32,256]{3,2,1,0:T(8,128)S(1)}) fusion(f32[32,32,256]{2,1,0:T(8,128)} %copy-done.12, f32[3,32,32,256]{3,2,1,0:T(8,128)} %copy-done.2, f32[32,32,256]{2,1,0:T(8,128)} %get-tuple-element.16, f32[3,32,32,1]{3,2,1,0:T(8,128)} %copy.189, f32[3,34,1,256]{3,2,1,0:T(1,128)S(1)} %pad.77, ...), kind=kLoop, calls=%fused_computation.308 | loop fusion | flops 38273024 | bytes 18255884 | tf_op jit(solution)/shard_map/reduce_sum | solution.py:65
  198.9 2.6 fusion.162
  201.7 2.7 copy.197
  204.4 7.6 %collective-permute-start.28 = (f32[3,32,32,1]{2,1,3,0:T(8,128)}, f32[3,32,32,1]{2,1,3,0:T(8,128)}, u32[]{:S(2)}, u32[]{:S(2)}) collective-permute-start(f32[3,32,32,1]{2,1,3,0:T(8,128)} %copy.197), channel_id=1, source_target_pairs={{0,1},{2,3},{4,5},{6,7},{8,9},{10,11},{12,13},{14,15},{16,17},{18,... | collective-permute-start | bytes 36872 | tf_op jit(solution)/shard_map/ppermute | solution.py:26
  213.6 2.6 copy.199
  218.2 4.9 collective-permute-start.26
  224.4 4.5 collective-permute-start.24
  231.7 2.7 copy.198
  234.4 2.6 copy.200
  238.3 10.9 %fusion.17 = f32[32,32,256]{2,1,0:T(8,128)S(1)} fusion(f32[3,32,32,256]{3,2,1,0:T(8,128)S(1)} %copy-done.7, f32[3,32,32,1]{3,2,1,0:T(8,128)} %copy.200, f32[3,34,1,256]{3,2,1,0:T(1,128)S(1)} %pad.81, f32[3,34,1,256]{3,2,1,0:T(1,128)S(1)} %pad.80, f32[3,1,32,256]{3,2,1,0:T(8,128)S(1)} %collective-permute-done.25, ...), kind=kLoop, calls=%fused_computation.22 | loop fusion | flops 34340864 | bytes 11964416 | tf_op jit(solution)/shard_map/reduce_sum | solution.py:170
  254.9 94.8 %all-gather.2.cloned.1.call-done = bf16[32,256,256]{2,1,0:T(8,128)(2,1)} async-done(((bf16[32,32,256]{2,1,0:T(8,128)(2,1)}), bf16[32,256,256]{2,1,0:T(8,128)(2,1)}) %all-gather.2.cloned.1.call-update) | async-done | bytes 4194320 | tf_op jit(solution)/shard_map/all_gather | solution.py:176
  349.7 6.0 %multiply_subtract_fusion.3 = f32[32,32,256]{2,1,0:T(8,128)} fusion(f32[32,32,256]{2,1,0:T(8,128)S(1)} %copy-done.16, f32[34,34,258]{2,1,0:T(8,128)S(1)} %copy-done.19, bf16[32,256,256]{2,1,0:T(8,128)(2,1)} %all-gather.2.cloned.1.call-done, bf16[32,256]{1,0:T(8,128)(2,1)S(1)} %copy-done), kind=kOutput, calls=%fused_computation.218 | convolution fusion | flops 147324928 | bytes 12599296 | tf_op jit(solution)/shard_map/yk,xkz->xyz/dot_general | solution.py:173
  355.8 3.8 reshape.339
  359.6 5.0 %copy.283 = f32[1,32,1,32,8,32]{5,3,1,4,2,0:T(8,128)} copy(f32[1,32,1,32,8,32]{5,4,3,1,2,0:T(8,128)} %reshape.339) | data formatting | bytes 2097152 | tf_op jit(solution)/shard_map/reshape | solution.py:114
  364.6 4.1 reshape_reshape.3
  368.7 1.9 convolution_bitcast_fusion.1
  370.6 2.6 copy.204
  373.1 6.8 %all-to-all-start = ((f32[16,1,32,1024]{3,2,1,0:T(8,128)}), f32[16,1,32,1024]{3,2,1,0:T(8,128)S(1)}, u32[]{:S(2)}, u32[]{:S(2)}) async-start(f32[16,1,32,1024]{3,2,1,0:T(8,128)} %copy.204), calls=%async_computation | async-start | bytes 4194304 | tf_op jit(solution)/shard_map/all_to_all | solution.py:213
  380.0 32.6 %all-to-all-done = f32[16,1,32,1024]{3,2,1,0:T(8,128)S(1)} async-done(((f32[16,1,32,1024]{3,2,1,0:T(8,128)}), f32[16,1,32,1024]{3,2,1,0:T(8,128)S(1)}, u32[]{:S(2)}, u32[]{:S(2)}) %all-to-all-start) | async-done | bytes 2097184 | tf_op jit(solution)/shard_map/all_to_all | solution.py:213
  412.6 2.0 fusion.101
  426.5 2.6 copy.230
  429.1 5.3 %all-to-all-start.1 = ((f32[16,1,32,1024]{3,2,1,0:T(8,128)}), f32[16,1,32,1024]{3,2,1,0:T(8,128)S(1)}, u32[]{:S(2)}, u32[]{:S(2)}) async-start(f32[16,1,32,1024]{3,2,1,0:T(8,128)} %copy.230), calls=%async_computation.1 | async-start | bytes 4194304 | tf_op jit(solution)/shard_map/all_to_all | solution.py:232
  434.4 3.8 reshape.351
  438.2 28.2 %all-to-all-done.1 = f32[16,1,32,1024]{3,2,1,0:T(8,128)S(1)} async-done(((f32[16,1,32,1024]{3,2,1,0:T(8,128)}), f32[16,1,32,1024]{3,2,1,0:T(8,128)S(1)}, u32[]{:S(2)}, u32[]{:S(2)}) %all-to-all-start.1) | async-done | bytes 2097184 | tf_op jit(solution)/shard_map/all_to_all | solution.py:232
  466.4 3.7 fusion.110
  470.1 3.9 reshape.346
  474.0 8.0 %copy.233 = f32[1,32,1,32,8,32]{5,4,3,1,2,0:T(8,128)} copy(f32[1,32,1,32,8,32]{5,3,4,1,2,0:T(8,128)} %bitcast.92) | data formatting | bytes 2097152 | tf_op jit(solution)/shard_map/transpose | solution.py:135
  482.0 4.2 reshape.347
  (188 shorter events, 55.8 us)
Async XLA Ops:
  7.2 342.6 %copy-start = (bf16[32,256]{1,0:T(8,128)(2,1)S(1)}, bf16[32,256]{1,0:T(8,128)(2,1)}, u32[]{:S(2)}) copy-start(bf16[32,256]{1,0:T(8,128)(2,1)} %param.13) | copy-start | bytes 49156
  7.2 14.5 %copy-start.20 = (s32[32,32,256]{2,1,0:T(8,128)S(1)}, s32[32,32,256]{2,1,0:T(8,128)}, u32[]{:S(2)}) copy-start(s32[32,32,256]{2,1,0:T(8,128)} %param.12) | copy-start | bytes 3145732
  7.2 342.5 %all-gather.2.cloned.1.call-start = ((), (), s32[]{:S(2)}) async-start(), calls=%async_computation.2 | async-start | bytes 4718592 | tf_op jit(solution)/shard_map/all_gather | solution.py:176
  7.2 14.5 %copy-start.18 = (f32[3,32,32,256]{3,2,1,0:T(8,128)S(1)}, f32[3,32,32,256]{3,2,1,0:T(8,128)}, u32[]{:S(2)}) copy-start(f32[3,32,32,256]{3,2,1,0:T(8,128)} %param.9) | copy-start | bytes 9437188
  8.7 13.0 %copy-start.13 = (bf16[32,32,256]{2,1,0:T(8,128)(2,1)}, bf16[32,32,256]{2,1,0:T(8,128)(2,1)S(1)}, u32[]{:S(2)}) copy-start(bf16[32,32,256]{2,1,0:T(8,128)(2,1)S(1)} %convert_element_type.45) | copy-start | bytes 1572868
  9.6 31.3 %collective-permute-start = (bf16[32,32,1]{2,1,0:T(8,128)(2,1)}, bf16[32,32,1]{2,1,0:T(8,128)(2,1)}, u32[]{:S(2)}, u32[]{:S(2)}) collective-permute-start(bf16[32,32,1]{2,1,0:T(8,128)(2,1)} %get-tuple-element.98), channel_id=1, source_target_pairs={{0,1},{2,3},{4,5},{6,7},{8,9},{10,11},{12,13},{14,15},{16,17},{18,... | collective-permute-start | bytes 6152 | tf_op jit(solution)/shard_map/ppermute | solution.py:26
  16.2 39.6 %collective-permute-start.5 = (bf16[32,32,1]{2,1,0:T(8,128)(2,1)S(1)}, bf16[32,32,1]{2,1,0:T(8,128)(2,1)}, u32[]{:S(2)}, u32[]{:S(2)}) collective-permute-start(bf16[32,32,1]{2,1,0:T(8,128)(2,1)S(1)} %get-tuple-element.99), channel_id=1, source_target_pairs={{1,0},{3,2},{5,4},{7,6},{9,8},{11,10},{13,12},{15,14},{17,16},{19,... | collective-permute-start | bytes 6152 | tf_op jit(solution)/shard_map/ppermute | solution.py:27
  18.1 40.9 %collective-permute-start.1 = (bf16[32,1,256]{2,1,0:T(2,128)(2,1)}, bf16[32,1,256]{2,1,0:T(2,128)(2,1)}, u32[]{:S(2)}, u32[]{:S(2)}) collective-permute-start(bf16[32,1,256]{2,1,0:T(2,128)(2,1)} %get-tuple-element.100), channel_id=1, source_target_pairs={{0,2},{2,4},{4,6},{6,8},{8,10},{10,12},{12,14},{1,3},{3,5},{5,7},{... | collective-permute-start | bytes 49160 | tf_op jit(solution)/shard_map/ppermute | solution.py:26
  21.8 1.7 copy-start.12
  23.4 23.4 %copy-start.4 = (f32[3,32,32,256]{3,2,1,0:T(8,128)}, f32[3,32,32,256]{3,2,1,0:T(8,128)S(1)}, u32[]{:S(2)}) copy-start(f32[3,32,32,256]{3,2,1,0:T(8,128)S(1)} %get-tuple-element.15) | copy-start | bytes 9437188
  28.7 13.5 %collective-permute-start.10 = (f32[3,32,32,1]{2,1,3,0:T(8,128)}, f32[3,32,32,1]{2,1,3,0:T(8,128)S(1)}, u32[]{:S(2)}, u32[]{:S(2)}) collective-permute-start(f32[3,32,32,1]{2,1,3,0:T(8,128)} %copy.166), channel_id=1, source_target_pairs={{0,1},{2,3},{4,5},{6,7},{8,9},{10,11},{12,13},{14,15},{16,17},{18,... | collective-permute-start | bytes 36872 | tf_op jit(solution)/shard_map/ppermute | solution.py:26
  38.1 7.5 %collective-permute-start.11 = (f32[3,32,32,1]{2,1,3,0:T(8,128)S(1)}, f32[3,32,32,1]{2,1,3,0:T(8,128)S(1)}, u32[]{:S(2)}, u32[]{:S(2)}) collective-permute-start(f32[3,32,32,1]{2,1,3,0:T(8,128)S(1)} %copy.168), channel_id=1, source_target_pairs={{1,0},{3,2},{5,4},{7,6},{9,8},{11,10},{13,12},{15,14},{17,16},{19,... | collective-permute-start | bytes 36872 | tf_op jit(solution)/shard_map/ppermute | solution.py:27
  40.9 19.5 %collective-permute-start.4 = (bf16[32,1,256]{2,1,0:T(2,128)(2,1)S(1)}, bf16[32,1,256]{2,1,0:T(2,128)(2,1)}, u32[]{:S(2)}, u32[]{:S(2)}) collective-permute-start(bf16[32,1,256]{2,1,0:T(2,128)(2,1)S(1)} %get-tuple-element.101), channel_id=1, source_target_pairs={{2,0},{4,2},{6,4},{8,6},{10,8},{12,10},{14,12},{3,1},{5,3},{7,5},{... | collective-permute-start | bytes 49160 | tf_op jit(solution)/shard_map/ppermute | solution.py:27
  42.2 6.1 %copy-start.21 = (f32[3,32,32,1]{2,1,3,0:T(8,128)}, f32[3,32,32,1]{2,1,3,0:T(8,128)S(1)}, u32[]{:S(2)}) copy-start(f32[3,32,32,1]{2,1,3,0:T(8,128)S(1)} %collective-permute-done.10) | copy-start | bytes 36868
  42.2 22.1 %collective-permute-start.2 = (bf16[1,32,256]{2,1,0:T(8,128)(2,1)}, bf16[1,32,256]{2,1,0:T(8,128)(2,1)}, u32[]{:S(2)}, u32[]{:S(2)}) collective-permute-start(bf16[1,32,256]{2,1,0:T(8,128)(2,1)} %get-tuple-element.102), channel_id=1, source_target_pairs={{0,16},{16,32},{32,48},{48,64},{64,80},{80,96},{96,112},{1,17},{17... | collective-permute-start | bytes 49160 | tf_op jit(solution)/shard_map/ppermute | solution.py:26
  45.5 2.7 copy-start.22
  45.6 20.0 %collective-permute-start.3 = (bf16[1,32,256]{2,1,0:T(8,128)(2,1)}, bf16[1,32,256]{2,1,0:T(8,128)(2,1)}, u32[]{:S(2)}, u32[]{:S(2)}) collective-permute-start(bf16[1,32,256]{2,1,0:T(8,128)(2,1)} %get-tuple-element.103), channel_id=1, source_target_pairs={{16,0},{32,16},{48,32},{64,48},{80,64},{96,80},{112,96},{17,1},{33... | collective-permute-start | bytes 49160 | tf_op jit(solution)/shard_map/ppermute | solution.py:27
  55.8 14.0 %copy-start.17 = (f32[32,32,256]{2,1,0:T(8,128)S(1)}, f32[32,32,256]{2,1,0:T(8,128)}, u32[]{:S(2)}) copy-start(f32[32,32,256]{2,1,0:T(8,128)} %get-tuple-element.14) | copy-start | bytes 3145732
  55.8 17.7 %collective-permute-start.8 = (f32[3,32,1,256]{3,1,2,0:T(8,128)}, f32[3,32,1,256]{3,1,2,0:T(8,128)S(1)}, u32[]{:S(2)}, u32[]{:S(2)}) collective-permute-start(f32[3,32,1,256]{3,1,2,0:T(8,128)} %copy.162), channel_id=1, source_target_pairs={{0,2},{2,4},{4,6},{6,8},{8,10},{10,12},{12,14},{1,3},{3,5},{5,7},{... | collective-permute-start | bytes 294920 | tf_op jit(solution)/shard_map/ppermute | solution.py:26
  59.0 14.7 %collective-permute-start.9 = (f32[3,32,1,256]{3,1,2,0:T(8,128)S(1)}, f32[3,32,1,256]{3,1,2,0:T(8,128)S(1)}, u32[]{:S(2)}, u32[]{:S(2)}) collective-permute-start(f32[3,32,1,256]{3,1,2,0:T(8,128)S(1)} %copy.164), channel_id=1, source_target_pairs={{2,0},{4,2},{6,4},{8,6},{10,8},{12,10},{14,12},{3,1},{5,3},{7,5},{... | collective-permute-start | bytes 294920 | tf_op jit(solution)/shard_map/ppermute | solution.py:27
  60.3 13.6 %collective-permute-start.6 = (f32[3,1,32,256]{3,2,1,0:T(8,128)}, f32[3,1,32,256]{3,2,1,0:T(8,128)S(1)}, u32[]{:S(2)}, u32[]{:S(2)}) collective-permute-start(f32[3,1,32,256]{3,2,1,0:T(8,128)} %get-tuple-element.47), channel_id=1, source_target_pairs={{0,16},{16,32},{32,48},{48,64},{64,80},{80,96},{96,112},{1,17},{17... | collective-permute-start | bytes 294920 | tf_op jit(solution)/shard_map/ppermute | solution.py:26
  64.3 9.7 %collective-permute-start.7 = (f32[3,1,32,256]{3,2,1,0:T(8,128)}, f32[3,1,32,256]{3,2,1,0:T(8,128)S(1)}, u32[]{:S(2)}, u32[]{:S(2)}) collective-permute-start(f32[3,1,32,256]{3,2,1,0:T(8,128)} %get-tuple-element.48), channel_id=1, source_target_pairs={{16,0},{32,16},{48,32},{64,48},{80,64},{96,80},{112,96},{17,1},{33... | collective-permute-start | bytes 294920 | tf_op jit(solution)/shard_map/ppermute | solution.py:27
  69.9 4.1 copy-start.5
  69.9 4.1 copy-start.23
  73.5 13.8 %copy-start.9 = (f32[32,32,256]{2,1,0:T(8,128)}, f32[32,32,256]{2,1,0:T(8,128)S(1)}, u32[]{:S(2)}) copy-start(f32[32,32,256]{2,1,0:T(8,128)S(1)} %get-tuple-element.18) | copy-start | bytes 3145732
  73.6 13.8 %copy-start.10 = (f32[32,32,256]{2,1,0:T(8,128)}, f32[32,32,256]{2,1,0:T(8,128)S(1)}, u32[]{:S(2)}) copy-start(f32[32,32,256]{2,1,0:T(8,128)S(1)} %get-tuple-element.19) | copy-start | bytes 3145732
  73.6 13.8 %copy-start.11 = (f32[32,32,256]{2,1,0:T(8,128)}, f32[32,32,256]{2,1,0:T(8,128)S(1)}, u32[]{:S(2)}) copy-start(f32[32,32,256]{2,1,0:T(8,128)S(1)} %get-tuple-element.20) | copy-start | bytes 3145732
  73.6 109.0 %copy-start.8 = (f32[32,32,256]{2,1,0:T(8,128)}, f32[32,32,256]{2,1,0:T(8,128)S(1)}, u32[]{:S(2)}) copy-start(f32[32,32,256]{2,1,0:T(8,128)S(1)} %get-tuple-element.17) | copy-start | bytes 3145732
  87.4 2.7 copy-start.3
  92.8 22.7 %collective-permute-start.16 = (f32[3,32,32,1]{2,1,3,0:T(8,128)}, f32[3,32,32,1]{2,1,3,0:T(8,128)}, u32[]{:S(2)}, u32[]{:S(2)}) collective-permute-start(f32[3,32,32,1]{2,1,3,0:T(8,128)} %copy.176), channel_id=1, source_target_pairs={{0,1},{2,3},{4,5},{6,7},{8,9},{10,11},{12,13},{14,15},{16,17},{18,... | collective-permute-start | bytes 36872 | tf_op jit(solution)/shard_map/ppermute | solution.py:26
  103.8 18.4 %collective-permute-start.17 = (f32[3,32,32,1]{2,1,3,0:T(8,128)}, f32[3,32,32,1]{2,1,3,0:T(8,128)}, u32[]{:S(2)}, u32[]{:S(2)}) collective-permute-start(f32[3,32,32,1]{2,1,3,0:T(8,128)} %copy.178), channel_id=1, source_target_pairs={{1,0},{3,2},{5,4},{7,6},{9,8},{11,10},{13,12},{15,14},{17,16},{19,... | collective-permute-start | bytes 36872 | tf_op jit(solution)/shard_map/ppermute | solution.py:27
  105.7 19.1 %collective-permute-start.14 = (f32[3,32,1,256]{3,1,2,0:T(8,128)}, f32[3,32,1,256]{3,1,2,0:T(8,128)}, u32[]{:S(2)}, u32[]{:S(2)}) collective-permute-start(f32[3,32,1,256]{3,1,2,0:T(8,128)} %copy.172), channel_id=1, source_target_pairs={{0,2},{2,4},{4,6},{6,8},{8,10},{10,12},{12,14},{1,3},{3,5},{5,7},{... | collective-permute-start | bytes 294920 | tf_op jit(solution)/shard_map/ppermute | solution.py:26
  110.0 15.9 %collective-permute-start.15 = (f32[3,32,1,256]{3,1,2,0:T(8,128)S(1)}, f32[3,32,1,256]{3,1,2,0:T(8,128)S(1)}, u32[]{:S(2)}, u32[]{:S(2)}) collective-permute-start(f32[3,32,1,256]{3,1,2,0:T(8,128)S(1)} %copy.174), channel_id=1, source_target_pairs={{2,0},{4,2},{6,4},{8,6},{10,8},{12,10},{14,12},{3,1},{5,3},{7,5},{... | collective-permute-start | bytes 294920 | tf_op jit(solution)/shard_map/ppermute | solution.py:27
  111.3 14.8 %collective-permute-start.12 = (f32[3,1,32,256]{3,2,1,0:T(8,128)}, f32[3,1,32,256]{3,2,1,0:T(8,128)S(1)}, u32[]{:S(2)}, u32[]{:S(2)}) collective-permute-start(f32[3,1,32,256]{3,2,1,0:T(8,128)} %get-tuple-element.41), channel_id=1, source_target_pairs={{0,16},{16,32},{32,48},{48,64},{64,80},{80,96},{96,112},{1,17},{17... | collective-permute-start | bytes 294920 | tf_op jit(solution)/shard_map/ppermute | solution.py:26
  115.6 10.5 %collective-permute-start.13 = (f32[3,1,32,256]{3,2,1,0:T(8,128)}, f32[3,1,32,256]{3,2,1,0:T(8,128)S(1)}, u32[]{:S(2)}, u32[]{:S(2)}) collective-permute-start(f32[3,1,32,256]{3,2,1,0:T(8,128)} %get-tuple-element.42), channel_id=1, source_target_pairs={{16,0},{32,16},{48,32},{64,48},{80,64},{96,80},{112,96},{17,1},{33... | collective-permute-start | bytes 294920 | tf_op jit(solution)/shard_map/ppermute | solution.py:27
  142.5 2.7 copy-start.2
  147.9 24.2 %collective-permute-start.22 = (f32[3,32,32,1]{2,1,3,0:T(8,128)}, f32[3,32,32,1]{2,1,3,0:T(8,128)}, u32[]{:S(2)}, u32[]{:S(2)}) collective-permute-start(f32[3,32,32,1]{2,1,3,0:T(8,128)} %copy.186), channel_id=1, source_target_pairs={{0,1},{2,3},{4,5},{6,7},{8,9},{10,11},{12,13},{14,15},{16,17},{18,... | collective-permute-start | bytes 36872 | tf_op jit(solution)/shard_map/ppermute | solution.py:26
  159.8 18.8 %collective-permute-start.23 = (f32[3,32,32,1]{2,1,3,0:T(8,128)}, f32[3,32,32,1]{2,1,3,0:T(8,128)}, u32[]{:S(2)}, u32[]{:S(2)}) collective-permute-start(f32[3,32,32,1]{2,1,3,0:T(8,128)} %copy.188), channel_id=1, source_target_pairs={{1,0},{3,2},{5,4},{7,6},{9,8},{11,10},{13,12},{15,14},{17,16},{19,... | collective-permute-start | bytes 36872 | tf_op jit(solution)/shard_map/ppermute | solution.py:27
  161.7 19.5 %collective-permute-start.20 = (f32[3,32,1,256]{3,1,2,0:T(8,128)}, f32[3,32,1,256]{3,1,2,0:T(8,128)}, u32[]{:S(2)}, u32[]{:S(2)}) collective-permute-start(f32[3,32,1,256]{3,1,2,0:T(8,128)} %copy.182), channel_id=1, source_target_pairs={{0,2},{2,4},{4,6},{6,8},{8,10},{10,12},{12,14},{1,3},{3,5},{5,7},{... | collective-permute-start | bytes 294920 | tf_op jit(solution)/shard_map/ppermute | solution.py:26
  166.3 16.0 %collective-permute-start.21 = (f32[3,32,1,256]{3,1,2,0:T(8,128)S(1)}, f32[3,32,1,256]{3,1,2,0:T(8,128)S(1)}, u32[]{:S(2)}, u32[]{:S(2)}) collective-permute-start(f32[3,32,1,256]{3,1,2,0:T(8,128)S(1)} %copy.184), channel_id=1, source_target_pairs={{2,0},{4,2},{6,4},{8,6},{10,8},{12,10},{14,12},{3,1},{5,3},{7,5},{... | collective-permute-start | bytes 294920 | tf_op jit(solution)/shard_map/ppermute | solution.py:27
  167.6 14.9 %collective-permute-start.18 = (f32[3,1,32,256]{3,2,1,0:T(8,128)}, f32[3,1,32,256]{3,2,1,0:T(8,128)S(1)}, u32[]{:S(2)}, u32[]{:S(2)}) collective-permute-start(f32[3,1,32,256]{3,2,1,0:T(8,128)} %get-tuple-element.35), channel_id=1, source_target_pairs={{0,16},{16,32},{32,48},{48,64},{64,80},{80,96},{96,112},{1,17},{17... | collective-permute-start | bytes 294920 | tf_op jit(solution)/shard_map/ppermute | solution.py:26
  172.2 10.4 %collective-permute-start.19 = (f32[3,1,32,256]{3,2,1,0:T(8,128)}, f32[3,1,32,256]{3,2,1,0:T(8,128)S(1)}, u32[]{:S(2)}, u32[]{:S(2)}) collective-permute-start(f32[3,1,32,256]{3,2,1,0:T(8,128)} %get-tuple-element.36), channel_id=1, source_target_pairs={{16,0},{32,16},{48,32},{64,48},{80,64},{96,80},{112,96},{17,1},{33... | collective-permute-start | bytes 294920 | tf_op jit(solution)/shard_map/ppermute | solution.py:27
  198.9 2.7 copy-start.6
  201.6 28.7 %copy-start.14 = (f32[32,32,256]{2,1,0:T(8,128)S(1)}, f32[32,32,256]{2,1,0:T(8,128)}, u32[]{:S(2)}) copy-start(f32[32,32,256]{2,1,0:T(8,128)} %get-tuple-element.8) | copy-start | bytes 3145732
  204.4 24.5 %collective-permute-start.28 = (f32[3,32,32,1]{2,1,3,0:T(8,128)}, f32[3,32,32,1]{2,1,3,0:T(8,128)}, u32[]{:S(2)}, u32[]{:S(2)}) collective-permute-start(f32[3,32,32,1]{2,1,3,0:T(8,128)} %copy.197), channel_id=1, source_target_pairs={{0,1},{2,3},{4,5},{6,7},{8,9},{10,11},{12,13},{14,15},{16,17},{18,... | collective-permute-start | bytes 36872 | tf_op jit(solution)/shard_map/ppermute | solution.py:26
  216.3 18.1 %collective-permute-start.29 = (f32[3,32,32,1]{2,1,3,0:T(8,128)}, f32[3,32,32,1]{2,1,3,0:T(8,128)}, u32[]{:S(2)}, u32[]{:S(2)}) collective-permute-start(f32[3,32,32,1]{2,1,3,0:T(8,128)} %copy.199), channel_id=1, source_target_pairs={{1,0},{3,2},{5,4},{7,6},{9,8},{11,10},{13,12},{15,14},{17,16},{19,... | collective-permute-start | bytes 36872 | tf_op jit(solution)/shard_map/ppermute | solution.py:27
  218.2 18.8 %collective-permute-start.26 = (f32[3,32,1,256]{3,1,2,0:T(8,128)}, f32[3,32,1,256]{3,1,2,0:T(8,128)}, u32[]{:S(2)}, u32[]{:S(2)}) collective-permute-start(f32[3,32,1,256]{3,1,2,0:T(8,128)} %copy.193), channel_id=1, source_target_pairs={{0,2},{2,4},{4,6},{6,8},{8,10},{10,12},{12,14},{1,3},{3,5},{5,7},{... | collective-permute-start | bytes 294920 | tf_op jit(solution)/shard_map/ppermute | solution.py:26
  223.1 15.0 %collective-permute-start.27 = (f32[3,32,1,256]{3,1,2,0:T(8,128)S(1)}, f32[3,32,1,256]{3,1,2,0:T(8,128)S(1)}, u32[]{:S(2)}, u32[]{:S(2)}) collective-permute-start(f32[3,32,1,256]{3,1,2,0:T(8,128)S(1)} %copy.195), channel_id=1, source_target_pairs={{2,0},{4,2},{6,4},{8,6},{10,8},{12,10},{14,12},{3,1},{5,3},{7,5},{... | collective-permute-start | bytes 294920 | tf_op jit(solution)/shard_map/ppermute | solution.py:27
  224.4 13.9 %collective-permute-start.24 = (f32[3,1,32,256]{3,2,1,0:T(8,128)}, f32[3,1,32,256]{3,2,1,0:T(8,128)S(1)}, u32[]{:S(2)}, u32[]{:S(2)}) collective-permute-start(f32[3,1,32,256]{3,2,1,0:T(8,128)} %get-tuple-element.27), channel_id=1, source_target_pairs={{0,16},{16,32},{32,48},{48,64},{64,80},{80,96},{96,112},{1,17},{17... | collective-permute-start | bytes 294920 | tf_op jit(solution)/shard_map/ppermute | solution.py:26
  229.0 9.3 %collective-permute-start.25 = (f32[3,1,32,256]{3,2,1,0:T(8,128)}, f32[3,1,32,256]{3,2,1,0:T(8,128)S(1)}, u32[]{:S(2)}, u32[]{:S(2)}) collective-permute-start(f32[3,1,32,256]{3,2,1,0:T(8,128)} %get-tuple-element.28), channel_id=1, source_target_pairs={{16,0},{32,16},{48,32},{64,48},{80,64},{96,80},{112,96},{17,1},{33... | collective-permute-start | bytes 294920 | tf_op jit(solution)/shard_map/ppermute | solution.py:27
  231.7 6.7 %copy-start.7 = (f32[3,32,32,256]{3,2,1,0:T(8,128)S(1)}, f32[3,32,32,256]{3,2,1,0:T(8,128)}, u32[]{:S(2)}) copy-start(f32[3,32,32,256]{3,2,1,0:T(8,128)} %copy-done.6) | copy-start | bytes 9437188
  238.3 10.9 %copy-start.15 = (f32[32,32,256]{2,1,0:T(8,128)S(1)}, f32[32,32,256]{2,1,0:T(8,128)}, u32[]{:S(2)}) copy-start(f32[32,32,256]{2,1,0:T(8,128)} %param.8) | copy-start | bytes 3145732
  249.2 5.5 %copy-start.24 = (s32[1,8]{1,0:T(1,128)S(1)}, s32[1,8]{1,0:T(1,128)}, u32[]{:S(2)}) copy-start(s32[1,8]{1,0:T(1,128)} %param.15) | copy-start | bytes 100
  249.2 100.5 %copy-start.16 = (f32[32,32,256]{2,1,0:T(8,128)S(1)}, f32[32,32,256]{2,1,0:T(8,128)}, u32[]{:S(2)}) copy-start(f32[32,32,256]{2,1,0:T(8,128)} %param.8) | copy-start | bytes 3145732
  249.3 100.5 %copy-start.19 = (f32[34,34,258]{2,1,0:T(8,128)S(1)}, f32[34,34,258]{2,1,0:T(8,128)}, u32[]{:S(2)}) copy-start(f32[34,34,258]{2,1,0:T(8,128)} %get-tuple-element.24) | copy-start | bytes 3578980
  373.1 39.5 %all-to-all-start = ((f32[16,1,32,1024]{3,2,1,0:T(8,128)}), f32[16,1,32,1024]{3,2,1,0:T(8,128)S(1)}, u32[]{:S(2)}, u32[]{:S(2)}) async-start(f32[16,1,32,1024]{3,2,1,0:T(8,128)} %copy.204), calls=%async_computation | async-start | bytes 4194304 | tf_op jit(solution)/shard_map/all_to_all | solution.py:213
  429.1 37.3 %all-to-all-start.1 = ((f32[16,1,32,1024]{3,2,1,0:T(8,128)}), f32[16,1,32,1024]{3,2,1,0:T(8,128)S(1)}, u32[]{:S(2)}, u32[]{:S(2)}) async-start(f32[16,1,32,1024]{3,2,1,0:T(8,128)} %copy.230), calls=%async_computation.1 | async-start | bytes 4194304 | tf_op jit(solution)/shard_map/all_to_all | solution.py:232
  474.0 12.2 %copy-start.1 = (bf16[32,256]{1,0:T(8,128)(2,1)S(1)}, bf16[32,256]{1,0:T(8,128)(2,1)}, u32[]{:S(2)}) copy-start(bf16[32,256]{1,0:T(8,128)(2,1)} %param.13) | copy-start | bytes 49156
Sparse Core Ops, SparseCore 0:
  250.4 99.2 all-gather.1
where the time goes:
time: 503 us; the launch traced here: 493 us
  waiting for transfers between devices  157 us (31%)
  local copies, waits for them, and re-layouts  112 us (22%)
  starting transfers between devices  107 us (21%)
  other arithmetic  87 us (17%)
  between operations  15.2 us (3%)
  matrix products  15.1 us (3%)
    all_gather x1, waiting for transfers between devices, local(): lax.all_gather(sensitivity, 'gy', axis=1, tiled=True)  94.8 us
    ppermute x15, starting transfers between devices, padded(): lax.ppermute(last, axis, up)  75.4 us
    reduce_sum x4, other arithmetic, operate(): result = coupling * centre_e[None] * jnp.sum(inner, axis=0, keepdims=True)  47.7 us
    slice x23, local copies, waits for them, and re-layouts, padded(): last = lax.slice_in_dim(x, length - width, length, axis=dim)  32.6 us
    all_to_all x1, waiting for transfers between devices, local(): lax.all_to_all(outgoing, ('gy', 'ga'), split_axis=0, concat_axis=0, tiled...  32.6 us
    all_to_all x1, waiting for transfers between devices, local(): lax.all_to_all(returning, ('gy', 'ga'), split_axis=0, concat_axis=0, tile...  28.2 us
    ppermute x15, starting transfers between devices, padded(): lax.ppermute(leading, axis, [(b, a) for a, b in up])  19.5 us
    ppermute x8, local copies, waits for them, and re-layouts, padded(): lax.ppermute(last, axis, up)  13.6 us
  transfers between devices with their start and end apart: 33, of which 4 were waited for; matrix products, arithmetic and copies ran while one was open for 16% of the time, Pallas kernels for 0%

commit v1 on v0

v1 whole, which is shorter than its diff:
```python
import jax
import jax.numpy as jnp
from jax import lax
from jax.experimental import pallas as pl
from jax.experimental.pallas import tpu as pltpu
from jax.sharding import PartitionSpec as P

TILE = 32
SWEEPS = 4
RELAX = 0.6
ADVANCE = 0.5
PSEUDO = 0.3
CX, CY, CZ = 32, 32, 256
NY = 256
ROWS = CX * CY
LANES = 128
CHUNK = 8
UNROLL = 3
TINY = 1e-37
F32, BF16 = jnp.float32, jnp.bfloat16
LIMIT = 8 << 20


SWAP_NEAR = [(i, i ^ 1) for i in range(8)]
SWAP_FAR = [(1, 2), (2, 1), (3, 4), (4, 3), (5, 6), (6, 5), (7, 0), (0, 7)]
SWAP_Z = [(0, 1), (1, 0)]

VM = pl.BlockSpec(memory_space=pltpu.VMEM)
SM = pl.BlockSpec(memory_space=pltpu.SMEM)
ANY = pl.BlockSpec(memory_space=pltpu.HBM)
HALVES = (slice(0, LANES), slice(LANES, 2 * LANES))


def shape(*dims, dtype=F32):
    return jax.ShapeDtypeStruct(dims, dtype)


def call(kernel, outs, scratch, args, specs=None, out_specs=None):
    return pl.pallas_call(
        kernel,
        out_shape=outs,
        in_specs=specs or [VM] * len(args),
        out_specs=out_specs or [VM] * len(outs),
        scratch_shapes=scratch,
        compiler_params=pltpu.CompilerParams(vmem_limit_bytes=LIMIT),
    )(*args)


class Place:
    def __init__(self):
        gx, gy, ga = lax.axis_index("gx"), lax.axis_index("gy"), lax.axis_index("ga")
        self.even_x, self.even_y = gx % 2 == 0, gy % 2 == 0
        self.x_lo = (gx > 0).astype(F32)
        self.x_hi = (gx < lax.axis_size("gx") - 1).astype(F32)
        self.y_lo = (gy > 0).astype(F32)
        self.y_hi = (gy < lax.axis_size("gy") - 1).astype(F32)
        self.first_z = ga == 0
        self.z_hi = (ga == 0).astype(F32)
        self.z_lo = (ga != 0).astype(F32)


def rows(x):
    return pl.ds(pl.multiple_of(x * CY, CY), CY)


def load(ref, x, half, *lead):
    return ref[(*lead, half, rows(x), slice(None))].reshape(4, 8, LANES)


def store(ref, x, half, value, *lead):
    ref[(*lead, half, rows(x), slice(None))] = value.reshape(CY, LANES)


def load_natural(ref, x, half, *lead):
    parts = [ref[(*lead, half, x, pl.ds(r, 8, stride=4), slice(None))] for r in range(4)]
    return jnp.stack([part.reshape(8, LANES) for part in parts])


def store_natural(ref, x, half, value, *lead):
    for r in range(4):
        ref[(*lead, half, x, pl.ds(r, 8, stride=4), slice(None))] = value[r]


def small_iotas():
    sub = lax.broadcasted_iota(jnp.int32, (8, LANES), 0)
    lane = lax.broadcasted_iota(jnp.int32, (4, 8, LANES), 2)
    return sub, lane


def y_sides(sub, tile, low, high):
    first = jnp.where(sub == 0, low, pltpu.roll(tile[3], 1, 0))
    last = jnp.where(sub == 7, high, pltpu.roll(tile[0], 7, 0))
    below = jnp.concatenate([first[None], tile[:3]], axis=0)
    above = jnp.concatenate([tile[1:], last[None]], axis=0)
    return below, above


def z_sides(lane, tiles, low, high):
    down = [pltpu.roll(tile, 1, 2) for tile in tiles]
    up = [pltpu.roll(tile, LANES - 1, 2) for tile in tiles]
    below = [jnp.where(lane == 0, low, down[0]), jnp.where(lane == 0, down[0], down[1])]
    above = [
        jnp.where(lane == LANES - 1, up[1], up[0]),
        jnp.where(lane == LANES - 1, high, up[1]),
    ]
    return below, above


def column(place, zh, index):
    target = jnp.where(place.first_z, LANES - 1, 0)
    return pltpu.roll(zh, lax.rem(target - index + 256, LANES), 1).reshape(4, 8, LANES)


def emit_faces(place, fields, xs, ys, zs):
    near_x = jnp.where(place.even_x, CX - 1, 0)
    near_y = jnp.where(place.even_y, CY - 1, 0)
    edge = jnp.where(place.first_z, 1, 0)
    source = jnp.where(place.first_z, LANES - 1, 0)
    for c, (ref, lead) in enumerate(fields):
        for turn in range(2):
            x = near_x if turn == 0 else CX - 1 - near_x
            y = near_y if turn == 0 else CY - 1 - near_y
            for half in range(2):
                plane = ref[(*lead, half, rows(x), slice(None))]
                side = ref[(*lead, half, pl.ds(y, CX, stride=CY), slice(None))]
                xs[turn][c, :, HALVES[half]] = plane.astype(BF16)
                ys[turn][c, :, HALVES[half]] = side.astype(BF16)
    lane = lax.broadcasted_iota(jnp.int32, (CY, LANES), 1)

    def step(block, total):
        for k in range(4):
            x = block * 4 + k
            for c, (ref, lead) in enumerate(fields):
                tile = ref[(*lead, edge, rows(x), slice(None))]
                index = c * CX + x
                moved = pltpu.roll(tile, lax.rem(index - source + LANES, LANES), 1)
                total = jnp.where(lane == index, moved, total)
        return total

    zs[...] = lax.fori_loop(0, CX // 4, step, jnp.zeros((CY, LANES), F32)).astype(BF16)


def stage_halos(place, rx, ry, xh, yh, count):
    for c in range(count):
        near, far = rx[0][c].astype(F32), rx[1][c].astype(F32)
        xh[0, c] = jnp.where(place.even_x, far, near)
        xh[1, c] = jnp.where(place.even_x, near, far)
        near, far = ry[0][c].astype(F32), ry[1][c].astype(F32)
        low, high = jnp.where(place.even_y, far, near), jnp.where(place.even_y, near, far)
        for h, half in enumerate(HALVES):
            yh[0, c, h] = low[:, half]
            yh[1, c, h] = high[:, half]


def plane_of(ref, *lead):
    return [ref[(*lead, slice(None), half)].reshape(4, 8, LANES) for half in HALVES]


def planes(ref, x, *lead):
    return [load(ref, x, half, *lead) for half in range(2)]


def over_planes(step, below_end, above_end, within):
    step(0, below_end, lambda c: within(c, 1))

    def inner(block, carry):
        for k in range(UNROLL):
            x = 1 + block * UNROLL + k
            step(x, lambda c: within(c, x - 1), lambda c: within(c, x + 1))
        return carry

    lax.fori_loop(0, (CX - 2) // UNROLL, inner, 0)
    step(CX - 1, lambda c: within(c, CX - 2), above_end)


def pack_kernel(
    prev, level, support, u0, lev, free, xs1, xs2, ys1, ys2, zs, prev_in, level_in, support_in, sems
):
    place = Place()
    copies = []
    for i in range(CX // CHUNK):
        part, trio = pl.ds(i * CHUNK, CHUNK), []
        for h, half in enumerate(HALVES):
            pairs = [(prev.at[c, part, :, half], prev_in.at[c, h, part]) for c in range(3)]
            pairs.append((level.at[part, :, half], level_in.at[h, part]))
            pairs.append((support.at[part, :, half], support_in.at[h, part]))
            for source, target in pairs:
                sem = sems.at[i, len(trio)]
                trio.append(pltpu.make_async_copy(source, target, sem))
        copies.append(trio)
    for trio in copies:
        for one in trio:
            one.start()
    for i, trio in enumerate(copies):
        for one in trio:
            one.wait()

        def step(block, carry):
            for k in range(2):
                x = i * CHUNK + block * 2 + k
                for half in range(2):
                    keep = (1 - load_natural(support_in, x, half)).astype(F32)
                    store(free, x, half, keep)
                    store(lev, x, half, load_natural(level_in, x, half))
                    for c in range(3):
                        store(u0, x, half, load_natural(prev_in, x, half, c) * keep, c)
            return carry

        lax.fori_loop(0, CHUNK // 2, step, 0)
    fields = [(u0, (c,)) for c in range(3)] + [(lev, ())]
    emit_faces(place, fields, (xs1, xs2), (ys1, ys2), zs)


def prepare_kernel(lev, load_mask, extension, tanh, loaded, turned, load_in, sem):
    copies = [
        pltpu.make_async_copy(load_mask.at[:, :, half], load_in.at[h], sem.at[h])
        for h, half in enumerate(HALVES)
    ]
    for one in copies:
        one.start()

    def bend(block, carry):
        for k in range(2):
            for half in range(2):
                x = block * 2 + k
                store(tanh, x, half, jnp.tanh(load(lev, x, half)))
        return carry

    lax.fori_loop(0, CX // 2, bend, 0)
    for one in copies:
        one.wait()

    def turn(block, carry):
        for k in range(2):
            x = block * 2 + k
            for half in range(2):
                store(loaded, x, half, load_natural(load_in, x, half).astype(F32))
        return carry

    lax.fori_loop(0, CX // 2, turn, 0)

    def order(size, along):
        place = lax.broadcasted_iota(jnp.int32, (size, size), along)
        other = lax.broadcasted_iota(jnp.int32, (size, size), 1 - along)
        source = place // CY * CY + place % 8 * 4 + place // 8 % 4
        return (source == other).astype(BF16)

    held = jnp.dot(order(CY, 0), extension[...], preferred_element_type=F32).astype(BF16)
    held = jnp.dot(held, order(NY, 1), preferred_element_type=F32)
    turned[...] = held.astype(BF16)


def sum_sides(place, sub, lane, x, u, yh, zh, x_below, x_above, weights):
    xl, xu, yl, yu, zl, zu = weights
    found = []
    for c in range(3):
        tiles = planes(u, x, c)
        side = column(place, zh, c * CX + x)
        z_below, z_above = z_sides(lane, tiles, side, side)
        x_lo, x_hi = x_below(c), x_above(c)
        sums = []
        for half in range(2):
            low, high = (yh[side, c, half, pl.ds(x, 8, stride=0), :] for side in range(2))
            y_below, y_above = y_sides(sub, tiles[half], low, high)
            total = xl[half] * x_lo[half] + xu[half] * x_hi[half]
            total = total + (yl[half] * y_below + yu[half] * y_above)
            total = total + (zl[half] * z_below[half] + zu[half] * z_above[half])
            sums.append(total)
        found.append((tiles, sums))
    return found


def first_kernel(
    traction, u, lev, free, tanh, loaded, rx1, rx2, ry1, ry2, rz,
    new, xs1, xs2, ys1, ys2, zs, wx, wyl, wyh, wzl, wzh, coup, diag, gain,
    xh, yh, zh,
):
    place = Place()
    sub, lane = small_iotas()
    stage_halos(place, (rx1, rx2), (ry1, ry2), xh, yh, 4)
    zh[0] = rz[...].astype(F32)
    bent = jnp.tanh(zh[0])
    zh[1] = bent * place.z_lo
    zh[2] = bent * place.z_hi
    yh[0, 3] = jnp.tanh(yh[0, 3]) * place.y_lo
    yh[1, 3] = jnp.tanh(yh[1, 3]) * place.y_hi
    xh[0, 3] = jnp.tanh(xh[0, 3]) * place.x_lo
    xh[1, 3] = jnp.tanh(xh[1, 3]) * place.x_hi
    row_mask = lax.broadcasted_iota(jnp.int32, (4, 8, LANES), 0) * 8 + sub[None]
    y_low = jnp.where(row_mask == 0, place.y_lo, 1.0)
    y_high = jnp.where(row_mask == CY - 1, place.y_hi, 1.0)
    z_low = [jnp.where(lane == 0, place.z_lo, 1.0), 1.0]
    z_high = [1.0, jnp.where(lane == LANES - 1, place.z_hi, 1.0)]

    def weight(a, b):
        return 0.525 + 0.2375 * (a + b)

    def step(x, x_below, x_above):
        centre = planes(tanh, x)
        z_below, z_above = z_sides(
            lane, centre, column(place, zh[1], 96 + x), column(place, zh[2], 96 + x)
        )
        t_below, t_above = x_below(3), x_above(3)
        kept, factors, totals, halves, forces = [[], [], [], [], [], []], [], [], [], []
        for half in range(2):
            mid = centre[half]
            low, high = (yh[side, 3, half, pl.ds(x, 8, stride=0), :] for side in range(2))
            y_below, y_above = y_sides(sub, mid, low, high)
            xl, xu = weight(mid, t_below[half]), weight(mid, t_above[half])
            yl, yu = weight(mid, y_below), weight(mid, y_above)
            zl, zu = weight(mid, z_below[half]), weight(mid, z_above[half])
            total = (xl + xu) + (yl + yu) + (zl + zu)
            middle = 0.2625 + 0.2375 * mid
            factor = RELAX * load(free, x, half) / (total + middle)
            yl, yu = yl * y_low, yu * y_high
            zl, zu = zl * z_low[half], zu * z_high[half]
            if isinstance(x, int) and x == 0:
                xl = xl * place.x_lo
                store(wx, 0, half, xl)
            if isinstance(x, int) and x == CX - 1:
                xu = xu * place.x_hi
            store(wx, x + 1, half, xu)
            store(wyl, x, half, yl)
            store(wyh, x, half, yu)
            store(wzl, x, half, zl)
            store(wzh, x, half, zu)
            store(coup, x, half, middle)
            store(diag, x, half, total)
            store(gain, x, half, factor)
            for into, one in zip(kept, (xl, xu, yl, yu, zl, zu)):
                into.append(one)
            factors.append(factor)
            totals.append(total)
            halves.append(middle)
            forces.append(load(loaded, x, half))
        found = sum_sides(place, sub, lane, x, u, yh, zh[0], x_below, x_above, kept)
        for half in range(2):
            shared = halves[half] * (found[0][0][half] + found[1][0][half] + found[2][0][half])
            for c in range(3):
                tile, near = found[c][0][half], found[c][1][half]
                push = near - shared + traction[c] * forces[half] - totals[half] * tile
                store(new, x, half, tile + factors[half] * push, c)

    over_planes(
        step,
        lambda c: plane_of(xh, 0, c),
        lambda c: plane_of(xh, 1, c),
        lambda c, x: planes(tanh, x) if c == 3 else planes(u, x, c),
    )
    emit_faces(place, [(new, (c,)) for c in range(3)], (xs1, xs2), (ys1, ys2), zs)


def sweep_kernel(
    traction, u, wx, wyl, wyh, wzl, wzh, coup, diag, gain, loaded, rx1, rx2, ry1, ry2, rz,
    new, xs1, xs2, ys1, ys2, zs, xh, yh, zh,
):
    place = Place()
    sub, lane = small_iotas()
    stage_halos(place, (rx1, rx2), (ry1, ry2), xh, yh, 3)
    zh[...] = rz[...].astype(F32)

    def step(x, x_below, x_above):
        weights = [planes(wx, x), planes(wx, x + 1)]
        weights += [planes(ref, x) for ref in (wyl, wyh, wzl, wzh)]
        found = sum_sides(place, sub, lane, x, u, yh, zh[...], x_below, x_above, weights)
        for half in range(2):
            shared = found[0][0][half] + found[1][0][half] + found[2][0][half]
            shared = load(coup, x, half) * shared
            factor, force, total = (load(ref, x, half) for ref in (gain, loaded, diag))
            for c in range(3):
                tile, near = found[c][0][half], found[c][1][half]
                push = near - shared + traction[c] * force - total * tile
                store(new, x, half, tile + factor * push, c)

    over_planes(
        step,
        lambda c: plane_of(xh, 0, c),
        lambda c: plane_of(xh, 1, c),
        lambda c, x: planes(u, x, c),
    )
    emit_faces(place, [(new, (c,)) for c in range(3)], (xs1, xs2), (ys1, ys2), zs)


def energy_kernel(
    u, tanh, wx, wyl, wyh, wzl, wzh, coup, diag, extension, rx1, rx2, ry1, ry2, rz,
    out, xh, yh, zh,
):
    place = Place()
    sub, lane = small_iotas()
    stage_halos(place, (rx1, rx2), (ry1, ry2), xh, yh, 3)
    zh[...] = rz[...].astype(F32)

    def step(x, x_below, x_above):
        weights = [planes(wx, x), planes(wx, x + 1)]
        weights += [planes(ref, x) for ref in (wyl, wyh, wzl, wzh)]
        found = sum_sides(place, sub, lane, x, u, yh, zh[...], x_below, x_above, weights)
        for half in range(2):
            shared = found[0][0][half] + found[1][0][half] + found[2][0][half]
            shared = load(coup, x, half) * shared
            total = load(diag, x, half)
            energy = jnp.zeros((4, 8, LANES), F32)
            for c in range(3):
                tile, near = found[c][0][half], found[c][1][half]
                energy = energy + tile * (total * tile + shared - near)
            bent = load(tanh, x, half)
            value = 0.5 * (1.0 - bent * bent) * energy
            out[x + x // 4, :, HALVES[half]] = value.reshape(CY, LANES).astype(BF16)

    over_planes(
        step,
        lambda c: plane_of(xh, 0, c),
        lambda c: plane_of(xh, 1, c),
        lambda c, x: planes(u, x, c),
    )
    for part in range(8):
        out[5 * part + 4] = extension[...]


def unpack_kernel(u, out, natural, sems):
    copies = []
    for c in range(3):

        def step(block, carry):
            for k in range(2):
                x = block * 2 + k
                for half in range(2):
                    store_natural(natural, x, half, load(u, x, half, c), c)
            return carry

        lax.fori_loop(0, CX // 2, step, 0)
        for h, half in enumerate(HALVES):
            one = pltpu.make_async_copy(natural.at[c, h], out.at[c, :, :, half], sems.at[c, h])
            one.start()
            copies.append(one)
    for one in copies:
        one.wait()


def product_kernel(received, out):
    matrix = jnp.concatenate([received[5 * part + 4] for part in range(8)], axis=0)
    for x in range(4):
        field = jnp.concatenate([received[5 * part + x] for part in range(8)], axis=0)
        moved = jnp.dot(matrix, field, preferred_element_type=F32).astype(BF16)
        for part in range(8):
            out[4 * part + x] = moved[CY * part : CY * (part + 1)]


def slopes_kernel(lev, rx1, rx2, ry1, ry2, rz, grow, shrink, xh, yh, zh):
    place = Place()
    sub, lane = small_iotas()
    near, far = rx1[3].astype(F32), rx2[3].astype(F32)
    xh[0] = jnp.where(place.even_x, far, near) * place.x_lo
    xh[1] = jnp.where(place.even_x, near, far) * place.x_hi
    near, far = ry1[3].astype(F32), ry2[3].astype(F32)
    low = jnp.where(place.even_y, far, near) * place.y_lo
    high = jnp.where(place.even_y, near, far) * place.y_hi
    for h, half in enumerate(HALVES):
        yh[0, h] = low[:, half]
        yh[1, h] = high[:, half]
    zh[0] = rz[...].astype(F32) * place.z_lo
    zh[1] = rz[...].astype(F32) * place.z_hi

    def step(x, x_below, x_above):
        centre = planes(lev, x)
        z_below, z_above = z_sides(
            lane, centre, column(place, zh[0], 96 + x), column(place, zh[1], 96 + x)
        )
        x_lo, x_hi = x_below(0), x_above(0)
        for half in range(2):
            mid = centre[half]
            low, high = (yh[side, half, pl.ds(x, 8, stride=0), :] for side in range(2))
            y_below, y_above = y_sides(sub, mid, low, high)
            growing = jnp.zeros((4, 8, LANES), F32)
            shrinking = jnp.zeros((4, 8, LANES), F32)
            pairs = ((x_lo[half], x_hi[half]), (y_below, y_above), (z_below[half], z_above[half]))
            for below, above in pairs:
                up = jnp.maximum(mid - jnp.minimum(below, above), 0.0)
                down = jnp.maximum(jnp.maximum(below, above) - mid, 0.0)
                growing = growing + up * up
                shrinking = shrinking + down * down
            store(grow, x, half, jnp.sqrt(growing))
            store(shrink, x, half, jnp.sqrt(shrinking))

    over_planes(
        step,
        lambda c: plane_of(xh, 0),
        lambda c: plane_of(xh, 1),
        lambda c, x: planes(lev, x),
    )


def final_kernel(
    counts, listing, lev, velocity, grow, shrink, out, first, second, sign, natural, sems
):
    gx, gy, ga = lax.axis_index("gx"), lax.axis_index("gy"), lax.axis_index("ga")
    sub, lane = small_iotas()
    own = counts[gx, gy * lax.axis_size("ga") + ga]
    listed = []
    for half in range(2):
        tile = lane[0] // TILE + half * (LANES // TILE)
        mask = jnp.zeros((8, LANES), F32)
        for entry in range(CZ // TILE):
            hit = jnp.where(entry < own, listing[0, entry], -1)
            mask = jnp.where(tile == hit, PSEUDO, mask)
        listed.append(mask)
    low_z, high_z = lane % TILE == 0, lane % TILE == TILE - 1

    def advance(block, carry):
        for k in range(2):
            x = block * 2 + k
            for half in range(2):
                moved = velocity[x, :, HALVES[half]].astype(F32).reshape(4, 8, LANES)
                speed = moved / (1.0 + jnp.abs(moved))
                change = jnp.maximum(speed, 0.0) * load(grow, x, half)
                change = change + jnp.minimum(speed, 0.0) * load(shrink, x, half)
                value = load(lev, x, half) - ADVANCE * change
                store(first, x, half, value)
                scaled = listed[half] * (value / jnp.sqrt(value * value + 1.0))
                store(sign, x, half, scaled)
        return carry

    lax.fori_loop(0, CX // 2, advance, 0)

    def sweep(source, x):
        done = []
        for half in range(2):
            centre = load(source, x, half)
            strength = load(sign, x, half)
            way = jnp.where(strength > 0.0, 1.0, -1.0)
            y_below, y_above = y_sides(sub, centre, centre[0], centre[3])
            sides = (
                (
                    load(source, jnp.maximum(x - 1, 0), half),
                    load(source, jnp.minimum(x + 1, CX - 1), half),
                ),
                (y_below, y_above),
                (
                    jnp.where(low_z, centre, pltpu.roll(centre, 1, 2)),
                    jnp.where(high_z, centre, pltpu.roll(centre, LANES - 1, 2)),
                ),
            )
            faced = way * centre
            total = None
            for below, above in sides:
                rise = jnp.maximum(faced - jnp.minimum(way * below, way * above), 0.0)
                total = rise * rise if total is None else total + rise * rise
            root = total * lax.rsqrt(jnp.maximum(total, TINY))
            done.append(centre - strength * (root - 1.0))
        return done

    buffers = [first, second]
    for turn in range(SWEEPS - 1):
        source, target = buffers[turn % 2], buffers[(turn + 1) % 2]

        def step(block, carry):
            for k in range(2):
                x = block * 2 + k
                for half, value in enumerate(sweep(source, x)):
                    store(target, x, half, value)
            return carry

        lax.fori_loop(0, CX // 2, step, 0)
    source = buffers[(SWEEPS - 1) % 2]
    copies = []
    for i in range(CX // CHUNK):

        def last(block, carry):
            for k in range(2):
                x = i * CHUNK + block * 2 + k
                for half, value in enumerate(sweep(source, x)):
                    store_natural(natural, x, half, value)
            return carry

        lax.fori_loop(0, CHUNK // 2, last, 0)
        part = pl.ds(i * CHUNK, CHUNK)
        for h, half in enumerate(HALVES):
            one = pltpu.make_async_copy(natural.at[h, part], out.at[part, :, half], sems.at[i, h])
            one.start()
            copies.append(one)
    for one in copies:
        one.wait()


def exchange(xs1, xs2, ys1, ys2, zs):
    return (
        lax.ppermute(xs1, "gx", SWAP_NEAR),
        lax.ppermute(xs2, "gx", SWAP_FAR),
        lax.ppermute(ys1, "gy", SWAP_NEAR),
        lax.ppermute(ys2, "gy", SWAP_FAR),
        lax.ppermute(zs, "ga", SWAP_Z),
    )


def faces(count):
    return [shape(count, 32, CZ, dtype=BF16)] * 4 + [shape(CY, LANES, dtype=BF16)]


def halo_scratch(count):
    return [pltpu.VMEM((2, count, CY, CZ), F32), pltpu.VMEM((2, count, 2, CX, LANES), F32)]


def local(
    level_set, displacement_prev, traction, load_mask, support_mask, extension, tile_count, tile_list
):
    displacement_prev, level_set, support_mask, load_mask = (
        pltpu.with_memory_space_constraint(x, pltpu.HBM)
        for x in (displacement_prev, level_set, support_mask, load_mask)
    )
    flat = shape(2, ROWS, LANES)
    field = shape(3, 2, ROWS, LANES)
    column_scratch = pltpu.VMEM((CY, LANES), F32)
    u, lev, free, *sent = call(
        pack_kernel,
        [field, flat, flat] + faces(4),
        [
            pltpu.VMEM((3, 2, CX, CY, LANES), F32),
            pltpu.VMEM((2, CX, CY, LANES), F32),
            pltpu.VMEM((2, CX, CY, LANES), jnp.int32),
            pltpu.SemaphoreType.DMA((CX // CHUNK, 10)),
        ],
        (displacement_prev, level_set, support_mask),
        [ANY] * 3,
    )
    got = exchange(*sent)
    level_got = got
    tanh, loaded, turned = call(
        prepare_kernel,
        [flat] * 2 + [shape(CY, NY, dtype=BF16)],
        [pltpu.VMEM((2, CX, CY, LANES), jnp.int32), pltpu.SemaphoreType.DMA((2,))],
        (lev, load_mask, extension),
        [VM, ANY, VM],
    )
    u, *rest = call(
        first_kernel,
        [field] + faces(3) + [shape(2, ROWS + CY, LANES)] + [flat] * 7,
        halo_scratch(4) + [pltpu.VMEM((3, CY, LANES), F32)],
        (traction, u, lev, free, tanh, loaded, *got),
        [SM] + [VM] * 10,
    )
    sent, made = rest[:5], rest[5:]
    got = exchange(*sent)
    grow, shrink = call(
        slopes_kernel, [flat] * 2,
        [pltpu.VMEM((2, CY, CZ), F32), pltpu.VMEM((2, 2, CX, LANES), F32)]
        + [pltpu.VMEM((2, CY, LANES), F32)],
        (lev, *level_got),
    )
    for turn in range(2):
        u, *sent = call(
            sweep_kernel, [field] + faces(3), halo_scratch(3) + [column_scratch],
            (traction, u, *made, loaded, *got),
            [SM] + [VM] * (len(made) + 7),
        )
        got = exchange(*sent)
    (displacement,) = call(
        unpack_kernel, [shape(3, CX, CY, CZ)],
        [pltpu.VMEM((3, 2, CX, CY, LANES), F32), pltpu.SemaphoreType.DMA((3, 2))],
        (u,), None, [ANY],
    )
    (sensitivity,) = call(
        energy_kernel, [shape(40, CY, CZ, dtype=BF16)], halo_scratch(3) + [column_scratch],
        (u, tanh, *made[:7], turned, *got),
    )
    sensitivity = lax.all_to_all(sensitivity, "gy", split_axis=0, concat_axis=0, tiled=True)
    (velocity,) = call(product_kernel, [shape(CX, CY, CZ, dtype=BF16)], [], (sensitivity,))
    velocity = lax.all_to_all(velocity, "gy", split_axis=0, concat_axis=0, tiled=True)
    (level_new,) = call(
        final_kernel, [shape(CX, CY, CZ)],
        [pltpu.VMEM((2, ROWS, LANES), F32)] * 3
        + [pltpu.VMEM((2, CX, CY, LANES), F32), pltpu.SemaphoreType.DMA((CX // CHUNK, 2))],
        (tile_count, tile_list, lev, velocity, grow, shrink),
        [SM, SM] + [VM] * 4,
        [ANY],
    )
    return (displacement, level_new)


def solution(mesh):
    return jax.shard_map(
        local,
        mesh=mesh,
        in_specs=(
            P("gx", "gy", "ga"),
            P(None, "gx", "gy", "ga"),
            P(),
            P("gx", "gy", "ga"),
            P("gx", "gy", "ga"),
            P("gy", None),
            P(),
            P(("gx", "gy", "ga"), None),
        ),
        out_specs=(P(None, "gx", "gy", "ga"), P("gx", "gy", "ga")),
        check_vma=False,
    )
```

time: 503 us -> 107 us (0.21); the launches traced: 493 us -> 106 us
  waiting for transfers between devices: 157 us -> 9.88 us
  local copies, waits for them, and re-layouts: 112 us -> 4.1 us
  other arithmetic: 87 us -> 0 us
  starting transfers between devices: 107 us -> 33.3 us
  Pallas kernels: 0 us -> 44.4 us
  matrix products: 15.1 us -> 0 us
  between operations: 15.2 us -> 0.85 us
  blocking collectives: 0 us -> 13.7 us
    all_gather x1 -> x0, waiting for transfers between devices: 94.8 us -> none  [local(): lax.all_gather(sensitivity, 'gy', axis=1, tiled=True)]
    ppermute x30 -> x20, starting transfers between devices: 94.9 us -> 29.8 us  [the longest x4 10.6 us: exchange(): lax.ppermute(zs, 'ga', SWAP_Z)]
    reduce_sum x7 -> x0, other arithmetic: 60.1 us -> none  [the longest x4 47.7 us: operate(): result = coupling * centre_e[None] * jnp.sum(inner, axis=0, keepdims=True)]
    all_to_all x2 -> x1, waiting for transfers between devices: 60.8 us -> 1.1 us  [local(): lax.all_to_all(velocity, 'gy', split_axis=0, concat_axis=0, tiled=True)]
    slice x55 -> x0, local copies, waits for them, and re-layouts: 45.7 us -> none  [the longest x23 32.6 us: padded(): last = lax.slice_in_dim(x, length - width, length, axis=dim)]
    pallas_call x0 -> x10, Pallas kernels: none -> 44.4 us  [call(): pl.pallas_call(kernel, out_shape=outs, in_specs=specs or [VM] * len(args)...]
    ppermute x16 -> x0, local copies, waits for them, and re-layouts: 24.4 us -> none  [the longest x8 13.6 us: padded(): lax.ppermute(last, axis, up)]
    reshape x5 -> x0, local copies, waits for them, and re-layouts: 20.7 us -> none  [the longest x2 8.82 us: into_tiles(): values.reshape(extent_x // tile_edge, tile_edge, extent_y // tile_edge, t...]
  transfers between devices with their start and end apart: 33 -> 21, of which waited for: 4 -> 4; matrix products, arithmetic and copies ran while one was open for 16% -> 0% of each run, Pallas kernels for 0% -> 5%
where the time goes in v1:
time: 107 us; the launch traced here: 106 us
  Pallas kernels  44.4 us (41%)
  starting transfers between devices  33.3 us (31%)
  blocking collectives  13.7 us (13%)
  waiting for transfers between devices  9.88 us (9%)
  local copies, waits for them, and re-layouts  4.1 us (4%)
    pallas_call x10, Pallas kernels, call(): pl.pallas_call(kernel, out_shape=outs, in_specs=specs or [VM] * len(args)...  44.4 us
    all_to_all x1, blocking collectives, local(): lax.all_to_all(sensitivity, 'gy', split_axis=0, concat_axis=0, tiled=True)  13.7 us
    ppermute x4, starting transfers between devices, exchange(): lax.ppermute(zs, 'ga', SWAP_Z)  10.6 us
    ppermute x4, starting transfers between devices, exchange(): lax.ppermute(ys2, 'gy', SWAP_FAR)  9.98 us
    ppermute x4, waiting for transfers between devices, exchange(): lax.ppermute(zs, 'ga', SWAP_Z)  8.75 us
    ppermute x4, starting transfers between devices, exchange(): lax.ppermute(xs2, 'gx', SWAP_FAR)  6.09 us
    unnamed x16, local copies, waits for them, and re-layouts  4.1 us
    all_to_all x1, starting transfers between devices, local(): lax.all_to_all(velocity, 'gy', split_axis=0, concat_axis=0, tiled=True)  3.49 us
  transfers between devices with their start and end apart: 21, of which 4 were waited for; matrix products, arithmetic and copies ran while one was open for 0% of the time, Pallas kernels for 5%

profile of v1, /device:TPU:0, one launch (start us, length us, event | category | flops | bytes accessed | tf_op | source)
XLA Modules:
  0.0 106.2 jit_solution(18256697991103175509)
XLA Ops:
  0.6 0.0 copy-start.4
  0.6 0.0 copy-start.5
  0.7 4.4 %shard_map.95 = (f32[3,2,1024,128]{3,2,1,0:T(8,128)S(1)}, f32[2,1024,128]{2,1,0:T(8,128)S(1)}, f32[2,1024,128]{2,1,0:T(8,128)S(1)}, bf16[4,32,256]{2,1,0:T(8,128...) custom-call(f32[3,32,32,256]{3,2,1,0:T(8,128)} %prev.1, ...), custom_call_target="tpu_custom_call" | custom-call | tf_op jit(solution)/shard_map/pallas_call | solution.py:39
  5.1 0.1 collective-permute-start
  5.1 3.0 %collective-permute-start.1 = (bf16[4,32,256]{2,1,0:T(8,128)(2,1)S(1)}, bf16[4,32,256]{2,1,0:T(8,128)(2,1)S(1)}, u32[]{:S(2)}, u32[]{:S(2)}) collective-permute-start(bf16[4,32,256]{2,1,0:T(8,128)(2,1)S(1)} %get-tuple-element.47), channel_id=1, source_target_pairs={{16,32},{32,16},{48,64},{64,48},{80,96},{96,80},{112,0},{0,112},{1... | collective-permute-start | bytes 196616 | tf_op jit(solution)/shard_map/ppermute | solution.py:587
  8.1 1.9 %collective-permute-start.2 = (bf16[4,32,256]{2,1,0:T(8,128)(2,1)S(1)}, bf16[4,32,256]{2,1,0:T(8,128)(2,1)S(1)}, u32[]{:S(2)}, u32[]{:S(2)}) collective-permute-start(bf16[4,32,256]{2,1,0:T(8,128)(2,1)S(1)} %get-tuple-element.48), channel_id=1, source_target_pairs={{0,2},{2,0},{4,6},{6,4},{8,10},{10,8},{12,14},{14,12},{1,3},{3,1},... | collective-permute-start | bytes 196616 | tf_op jit(solution)/shard_map/ppermute | solution.py:588
  10.0 2.6 %collective-permute-start.3 = (bf16[4,32,256]{2,1,0:T(8,128)(2,1)S(1)}, bf16[4,32,256]{2,1,0:T(8,128)(2,1)S(1)}, u32[]{:S(2)}, u32[]{:S(2)}) collective-permute-start(bf16[4,32,256]{2,1,0:T(8,128)(2,1)S(1)} %get-tuple-element.49), channel_id=1, source_target_pairs={{2,4},{4,2},{6,8},{8,6},{10,12},{12,10},{14,0},{0,14},{3,5},{5,3},... | collective-permute-start | bytes 196616 | tf_op jit(solution)/shard_map/ppermute | solution.py:589
  12.6 3.9 %collective-permute-start.4 = (bf16[32,128]{1,0:T(8,128)(2,1)S(1)}, bf16[32,128]{1,0:T(8,128)(2,1)S(1)}, u32[]{:S(2)}, u32[]{:S(2)}) collective-permute-start(bf16[32,128]{1,0:T(8,128)(2,1)S(1)} %get-tuple-element.50), channel_id=1, source_target_pairs={{0,1},{1,0},{2,3},{3,2},{4,5},{5,4},{6,7},{7,6},{8,9},{9,8},{10,11... | collective-permute-start | bytes 24584 | tf_op jit(solution)/shard_map/ppermute | solution.py:590
  16.5 0.0 copy-done.4
  16.5 1.6 %shard_map.96 = (f32[2,1024,128]{2,1,0:T(8,128)S(1)}, f32[2,1024,128]{2,1,0:T(8,128)S(1)}, bf16[32,256]{1,0:T(8,128)(2,1)S(1)}) custom-call(f32[2,1024,128]{2,1,0:T(8,128)S(1)} %get-tuple-element.42.lev, s32[32,32,256]{2,1,0:T(8,128)} %load_mask.1, bf16[32,256]{1,0:T(8,128)(2,1)S(1)} %copy-done.4), custom_call_target="tpu_custom_call" | custom-call | tf_op jit(solution)/shard_map/pallas_call | solution.py:39
  18.1 0.0 collective-permute-done.4.rz
  18.1 0.0 collective-permute-done.rx1
  18.1 0.0 collective-permute-done.1.rx2
  18.1 0.0 collective-permute-done.2.ry1
  18.1 0.0 collective-permute-done.3.ry2
  18.1 0.0 copy-done.5
  18.1 6.8 %shard_map.97 = (f32[3,2,1024,128]{3,2,1,0:T(8,128)S(1)}, bf16[3,32,256]{2,1,0:T(8,128)(2,1)S(1)}, bf16[3,32,256]{2,1,0:T(8,128)(2,1)S(1)}, bf16[3,32,256]{2,1,0...) custom-call(f32[3]{0:T(128)S(1)} %copy-done.5, ...), custom_call_target="tpu_custom_call" | custom-call | tf_op jit(solution)/shard_map/pallas_call | solution.py:39
  24.9 0.1 collective-permute-start.5
  25.0 0.9 collective-permute-start.6
  26.0 0.1 collective-permute-start.7
  26.1 2.2 %collective-permute-start.8 = (bf16[3,32,256]{2,1,0:T(8,128)(2,1)S(1)}, bf16[3,32,256]{2,1,0:T(8,128)(2,1)S(1)}, u32[]{:S(2)}, u32[]{:S(2)}) collective-permute-start(bf16[3,32,256]{2,1,0:T(8,128)(2,1)S(1)} %get-tuple-element.63), channel_id=1, source_target_pairs={{2,4},{4,2},{6,8},{8,6},{10,12},{12,10},{14,0},{0,14},{3,5},{5,3},... | collective-permute-start | bytes 147464 | tf_op jit(solution)/shard_map/ppermute | solution.py:589
  28.3 3.4 %collective-permute-start.9 = (bf16[32,128]{1,0:T(8,128)(2,1)S(1)}, bf16[32,128]{1,0:T(8,128)(2,1)S(1)}, u32[]{:S(2)}, u32[]{:S(2)}) collective-permute-start(bf16[32,128]{1,0:T(8,128)(2,1)S(1)} %get-tuple-element.64), channel_id=1, source_target_pairs={{0,1},{1,0},{2,3},{3,2},{4,5},{5,4},{6,7},{7,6},{8,9},{9,8},{10,11... | collective-permute-start | bytes 24584 | tf_op jit(solution)/shard_map/ppermute | solution.py:590
  31.7 1.7 %collective-permute-done.9.rz = bf16[32,128]{1,0:T(8,128)(2,1)S(1)} collective-permute-done((bf16[32,128]{1,0:T(8,128)(2,1)S(1)}, bf16[32,128]{1,0:T(8,128)(2,1)S(1)}, u32[]{:S(2)}, u32[]{:S(2)}) %collective-permute-start.9) | collective-permute-done | bytes 8224 | tf_op jit(solution)/shard_map/ppermute | solution.py:590
  33.4 0.0 collective-permute-done.5.rx1
  33.4 0.0 collective-permute-done.6.rx2
  33.5 0.0 collective-permute-done.7.ry1
  33.5 0.0 collective-permute-done.8.ry2
  33.5 6.0 %shard_map.98 = (f32[3,2,1024,128]{3,2,1,0:T(8,128)S(1)}, bf16[3,32,256]{2,1,0:T(8,128)(2,1)S(1)}, bf16[3,32,256]{2,1,0:T(8,128)(2,1)S(1)}, bf16[3,32,256]{2,1,0...) custom-call(f32[3]{0:T(128)S(1)} %copy-done.5, ...), custom_call_target="tpu_custom_call" | custom-call | tf_op jit(solution)/shard_map/pallas_call | solution.py:39
  39.5 0.1 collective-permute-start.10
  39.6 1.2 %collective-permute-start.11 = (bf16[3,32,256]{2,1,0:T(8,128)(2,1)S(1)}, bf16[3,32,256]{2,1,0:T(8,128)(2,1)S(1)}, u32[]{:S(2)}, u32[]{:S(2)}) collective-permute-start(bf16[3,32,256]{2,1,0:T(8,128)(2,1)S(1)} %get-tuple-element.67), channel_id=1, source_target_pairs={{16,32},{32,16},{48,64},{64,48},{80,96},{96,80},{112,0},{0,112},{1... | collective-permute-start | bytes 147464 | tf_op jit(solution)/shard_map/ppermute | solution.py:587
  40.8 0.6 collective-permute-start.12
  41.4 3.4 %collective-permute-start.13 = (bf16[3,32,256]{2,1,0:T(8,128)(2,1)S(1)}, bf16[3,32,256]{2,1,0:T(8,128)(2,1)S(1)}, u32[]{:S(2)}, u32[]{:S(2)}) collective-permute-start(bf16[3,32,256]{2,1,0:T(8,128)(2,1)S(1)} %get-tuple-element.69), channel_id=1, source_target_pairs={{2,4},{4,2},{6,8},{8,6},{10,12},{12,10},{14,0},{0,14},{3,5},{5,3},... | collective-permute-start | bytes 147464 | tf_op jit(solution)/shard_map/ppermute | solution.py:589
  44.8 1.5 %collective-permute-start.14 = (bf16[32,128]{1,0:T(8,128)(2,1)S(1)}, bf16[32,128]{1,0:T(8,128)(2,1)S(1)}, u32[]{:S(2)}, u32[]{:S(2)}) collective-permute-start(bf16[32,128]{1,0:T(8,128)(2,1)S(1)} %get-tuple-element.70), channel_id=1, source_target_pairs={{0,1},{1,0},{2,3},{3,2},{4,5},{5,4},{6,7},{7,6},{8,9},{9,8},{10,11... | collective-permute-start | bytes 24584 | tf_op jit(solution)/shard_map/ppermute | solution.py:590
  46.3 3.6 %collective-permute-done.14.rz = bf16[32,128]{1,0:T(8,128)(2,1)S(1)} collective-permute-done((bf16[32,128]{1,0:T(8,128)(2,1)S(1)}, bf16[32,128]{1,0:T(8,128)(2,1)S(1)}, u32[]{:S(2)}, u32[]{:S(2)}) %collective-permute-start.14) | collective-permute-done | bytes 8224 | tf_op jit(solution)/shard_map/ppermute | solution.py:590
  49.9 0.0 collective-permute-done.10.rx1
  49.9 0.0 collective-permute-done.11.rx2
  49.9 0.0 collective-permute-done.12.ry1
  49.9 0.0 collective-permute-done.13.ry2
  49.9 6.0 %shard_map.99 = (f32[3,2,1024,128]{3,2,1,0:T(8,128)S(1)}, bf16[3,32,256]{2,1,0:T(8,128)(2,1)S(1)}, bf16[3,32,256]{2,1,0:T(8,128)(2,1)S(1)}, bf16[3,32,256]{2,1,0...) custom-call(f32[3]{0:T(128)S(1)} %copy-done.5, ...), custom_call_target="tpu_custom_call" | custom-call | tf_op jit(solution)/shard_map/pallas_call | solution.py:39
  56.0 0.0 copy-start
  56.0 0.1 collective-permute-start.15
  56.1 1.0 collective-permute-start.16
  57.0 0.2 collective-permute-start.17
  57.2 1.9 %collective-permute-start.18 = (bf16[3,32,256]{2,1,0:T(8,128)(2,1)S(1)}, bf16[3,32,256]{2,1,0:T(8,128)(2,1)S(1)}, u32[]{:S(2)}, u32[]{:S(2)}) collective-permute-start(bf16[3,32,256]{2,1,0:T(8,128)(2,1)S(1)} %get-tuple-element.76), channel_id=1, source_target_pairs={{2,4},{4,2},{6,8},{8,6},{10,12},{12,10},{14,0},{0,14},{3,5},{5,3},... | collective-permute-start | bytes 147464 | tf_op jit(solution)/shard_map/ppermute | solution.py:589
  59.0 1.8 %collective-permute-start.19 = (bf16[32,128]{1,0:T(8,128)(2,1)S(1)}, bf16[32,128]{1,0:T(8,128)(2,1)S(1)}, u32[]{:S(2)}, u32[]{:S(2)}) collective-permute-start(bf16[32,128]{1,0:T(8,128)(2,1)S(1)} %get-tuple-element.77), channel_id=1, source_target_pairs={{0,1},{1,0},{2,3},{3,2},{4,5},{5,4},{6,7},{7,6},{8,9},{9,8},{10,11... | collective-permute-start | bytes 24584 | tf_op jit(solution)/shard_map/ppermute | solution.py:590
  60.8 3.4 %collective-permute-done.19.rz = bf16[32,128]{1,0:T(8,128)(2,1)S(1)} collective-permute-done((bf16[32,128]{1,0:T(8,128)(2,1)S(1)}, bf16[32,128]{1,0:T(8,128)(2,1)S(1)}, u32[]{:S(2)}, u32[]{:S(2)}) %collective-permute-start.19) | collective-permute-done | bytes 8224 | tf_op jit(solution)/shard_map/ppermute | solution.py:590
  64.2 0.0 collective-permute-done.15.rx1
  64.2 0.0 collective-permute-done.16.rx2
  64.2 0.0 collective-permute-done.17.ry1
  64.2 0.0 collective-permute-done.18.ry2
  64.2 4.1 %shard_map.101 = bf16[40,32,256]{2,1,0:T(8,128)(2,1)S(1)} custom-call(f32[3,2,1024,128]{3,2,1,0:T(8,128)S(1)} %get-tuple-element.71.u, f32[2,1024,128]{2,1,0:T(8,128)S(1)} %get-tuple-element.44.tanh, f32[2,1056,128]{2,1,0:T(8,128)S(1)} %get-tuple-element.52.wx, f32[2,1024,128]{2,1,0:T(8,128)S(1)} %get-tuple-element.53.wyl, ...), custom_call_target="tpu_custom_call" | custom-call | tf_op jit(solution)/shard_map/pallas_call | solution.py:39
  68.4 0.0 copy-done
  68.4 13.7 %all_to_all.10.received = bf16[40,32,256]{2,1,0:T(8,128)(2,1)S(1)} all-to-all(bf16[40,32,256]{2,1,0:T(8,128)(2,1)S(1)} %shard_map.101), channel_id=1, replica_groups=mesh['gx'=8,'gy'=8,'ga'=2] {'gy'}, dimensions={0} | all-to-all | bytes 1310720 | tf_op jit(solution)/shard_map/all_to_all | solution.py:664
  82.1 1.1 %shard_map.102 = bf16[32,32,256]{2,1,0:T(8,128)(2,1)} custom-call(bf16[40,32,256]{2,1,0:T(8,128)(2,1)S(1)} %all_to_all.10.received), custom_call_target="tpu_custom_call" | custom-call | tf_op jit(solution)/shard_map/pallas_call | solution.py:39
  83.2 3.5 %all-to-all-start.1 = ((bf16[32,32,256]{2,1,0:T(8,128)(2,1)}), bf16[32,32,256]{2,1,0:T(8,128)(2,1)S(1)}, u32[]{:S(2)}, u32[]{:S(2)}) async-start(bf16[32,32,256]{2,1,0:T(8,128)(2,1)} %shard_map.102), calls=%async_computation.1 | async-start | bytes 1048576 | tf_op jit(solution)/shard_map/all_to_all | solution.py:666
  86.7 2.3 %shard_map.103 = (f32[2,1024,128]{2,1,0:T(8,128)S(1)}, f32[2,1024,128]{2,1,0:T(8,128)S(1)}) custom-call(f32[2,1024,128]{2,1,0:T(8,128)S(1)} %get-tuple-element.42.lev, bf16[4,32,256]{2,1,0:T(8,128)(2,1)S(1)} %collective-permute-done.rx1, bf16[4,32,256]{2,1,0:T(8,128)(2,1)S(1)} %collective-permute-done.1.rx2, ...), custom_call_target="tpu_custom_call" | custom-call | tf_op jit(solution)/shard_map/pallas_call | solution.py:39
  88.9 0.0 copy-start.2
  89.0 1.0 copy-done.2
  89.9 1.9 %copy-done.1 = f32[3,2,1024,128]{3,2,1,0:T(8,128)S(1)} copy-done((f32[3,2,1024,128]{3,2,1,0:T(8,128)S(1)}, f32[3,2,1024,128]{3,2,1,0:T(8,128)}, u32[]{:S(2)}) %copy-start.1) | copy-done | bytes 3145752
  91.8 1.8 %shard_map.100 = f32[3,32,32,256]{3,2,1,0:T(8,128)} custom-call(f32[3,2,1024,128]{3,2,1,0:T(8,128)S(1)} %copy-done.1), custom_call_target="tpu_custom_call" | custom-call | tf_op jit(solution)/shard_map/pallas_call | solution.py:39
  93.7 1.1 %all-to-all-done.1.velocity = bf16[32,32,256]{2,1,0:T(8,128)(2,1)S(1)} async-done(((bf16[32,32,256]{2,1,0:T(8,128)(2,1)}), bf16[32,32,256]{2,1,0:T(8,128)(2,1)S(1)}, u32[]{:S(2)}, u32[]{:S(2)}) %all-to-all-start.1) | async-done | bytes 524320 | tf_op jit(solution)/shard_map/all_to_all | solution.py:666
  94.8 0.0 copy-done.6
  94.8 1.2 %copy-done.3 = f32[2,1024,128]{2,1,0:T(8,128)S(1)} copy-done((f32[2,1024,128]{2,1,0:T(8,128)S(1)}, f32[2,1024,128]{2,1,0:T(8,128)}, u32[]{:S(2)}) %copy-start.3) | copy-done | bytes 1048600
  96.0 10.2 %shard_map.104 = f32[32,32,256]{2,1,0:T(8,128)} custom-call(s32[8,16]{1,0:T(8,128)S(1)} %copy-done.6, s32[1,8]{1,0:T(1,128)S(1)} %copy-done.7, f32[2,1024,128]{2,1,0:T(8,128)S(1)} %get-tuple-element.42.lev, bf16[32,32,256]{2,1,0:T(8,128)(2,1)S(1)} %all-to-all-done.1.velocity, f32[2,1024,128]{2,1,0:T(8,128)S(1)} %get-tuple-element.78.grow, ...), custom_call_target="tpu_custom_call" | custom-call | tf_op jit(solution)/shard_map/pallas_call | solution.py:39
  (5 shorter events, 0.0 us)
Async XLA Ops:
  0.6 15.8 %copy-start.4 = (bf16[32,256]{1,0:T(8,128)(2,1)S(1)}, bf16[32,256]{1,0:T(8,128)(2,1)}, u32[]{:S(2)}) copy-start(bf16[32,256]{1,0:T(8,128)(2,1)} %extension.1) | copy-start | bytes 49156
  0.6 17.5 %copy-start.5 = (f32[3]{0:T(128)S(1)}, f32[3]{0:T(128)}, u32[]{:S(2)}) copy-start(f32[3]{0:T(128)} %traction.5) | copy-start | bytes 40
  5.1 13.1 %collective-permute-start = (bf16[4,32,256]{2,1,0:T(8,128)(2,1)S(1)}, bf16[4,32,256]{2,1,0:T(8,128)(2,1)S(1)}, u32[]{:S(2)}, u32[]{:S(2)}) collective-permute-start(bf16[4,32,256]{2,1,0:T(8,128)(2,1)S(1)} %get-tuple-element.46), channel_id=1, source_target_pairs={{0,16},{16,0},{32,48},{48,32},{64,80},{80,64},{96,112},{112,96},{1... | collective-permute-start | bytes 196616 | tf_op jit(solution)/shard_map/ppermute | solution.py:586
  5.1 13.0 %collective-permute-start.1 = (bf16[4,32,256]{2,1,0:T(8,128)(2,1)S(1)}, bf16[4,32,256]{2,1,0:T(8,128)(2,1)S(1)}, u32[]{:S(2)}, u32[]{:S(2)}) collective-permute-start(bf16[4,32,256]{2,1,0:T(8,128)(2,1)S(1)} %get-tuple-element.47), channel_id=1, source_target_pairs={{16,32},{32,16},{48,64},{64,48},{80,96},{96,80},{112,0},{0,112},{1... | collective-permute-start | bytes 196616 | tf_op jit(solution)/shard_map/ppermute | solution.py:587
  8.1 10.0 %collective-permute-start.2 = (bf16[4,32,256]{2,1,0:T(8,128)(2,1)S(1)}, bf16[4,32,256]{2,1,0:T(8,128)(2,1)S(1)}, u32[]{:S(2)}, u32[]{:S(2)}) collective-permute-start(bf16[4,32,256]{2,1,0:T(8,128)(2,1)S(1)} %get-tuple-element.48), channel_id=1, source_target_pairs={{0,2},{2,0},{4,6},{6,4},{8,10},{10,8},{12,14},{14,12},{1,3},{3,1},... | collective-permute-start | bytes 196616 | tf_op jit(solution)/shard_map/ppermute | solution.py:588
  10.0 8.1 %collective-permute-start.3 = (bf16[4,32,256]{2,1,0:T(8,128)(2,1)S(1)}, bf16[4,32,256]{2,1,0:T(8,128)(2,1)S(1)}, u32[]{:S(2)}, u32[]{:S(2)}) collective-permute-start(bf16[4,32,256]{2,1,0:T(8,128)(2,1)S(1)} %get-tuple-element.49), channel_id=1, source_target_pairs={{2,4},{4,2},{6,8},{8,6},{10,12},{12,10},{14,0},{0,14},{3,5},{5,3},... | collective-permute-start | bytes 196616 | tf_op jit(solution)/shard_map/ppermute | solution.py:589
  12.6 5.5 %collective-permute-start.4 = (bf16[32,128]{1,0:T(8,128)(2,1)S(1)}, bf16[32,128]{1,0:T(8,128)(2,1)S(1)}, u32[]{:S(2)}, u32[]{:S(2)}) collective-permute-start(bf16[32,128]{1,0:T(8,128)(2,1)S(1)} %get-tuple-element.50), channel_id=1, source_target_pairs={{0,1},{1,0},{2,3},{3,2},{4,5},{5,4},{6,7},{7,6},{8,9},{9,8},{10,11... | collective-permute-start | bytes 24584 | tf_op jit(solution)/shard_map/ppermute | solution.py:590
  24.9 8.5 %collective-permute-start.5 = (bf16[3,32,256]{2,1,0:T(8,128)(2,1)S(1)}, bf16[3,32,256]{2,1,0:T(8,128)(2,1)S(1)}, u32[]{:S(2)}, u32[]{:S(2)}) collective-permute-start(bf16[3,32,256]{2,1,0:T(8,128)(2,1)S(1)} %get-tuple-element.60), channel_id=1, source_target_pairs={{0,16},{16,0},{32,48},{48,32},{64,80},{80,64},{96,112},{112,96},{1... | collective-permute-start | bytes 147464 | tf_op jit(solution)/shard_map/ppermute | solution.py:586
  25.0 8.4 %collective-permute-start.6 = (bf16[3,32,256]{2,1,0:T(8,128)(2,1)S(1)}, bf16[3,32,256]{2,1,0:T(8,128)(2,1)S(1)}, u32[]{:S(2)}, u32[]{:S(2)}) collective-permute-start(bf16[3,32,256]{2,1,0:T(8,128)(2,1)S(1)} %get-tuple-element.61), channel_id=1, source_target_pairs={{16,32},{32,16},{48,64},{64,48},{80,96},{96,80},{112,0},{0,112},{1... | collective-permute-start | bytes 147464 | tf_op jit(solution)/shard_map/ppermute | solution.py:587
  26.0 7.5 %collective-permute-start.7 = (bf16[3,32,256]{2,1,0:T(8,128)(2,1)S(1)}, bf16[3,32,256]{2,1,0:T(8,128)(2,1)S(1)}, u32[]{:S(2)}, u32[]{:S(2)}) collective-permute-start(bf16[3,32,256]{2,1,0:T(8,128)(2,1)S(1)} %get-tuple-element.62), channel_id=1, source_target_pairs={{0,2},{2,0},{4,6},{6,4},{8,10},{10,8},{12,14},{14,12},{1,3},{3,1},... | collective-permute-start | bytes 147464 | tf_op jit(solution)/shard_map/ppermute | solution.py:588
  26.1 7.4 %collective-permute-start.8 = (bf16[3,32,256]{2,1,0:T(8,128)(2,1)S(1)}, bf16[3,32,256]{2,1,0:T(8,128)(2,1)S(1)}, u32[]{:S(2)}, u32[]{:S(2)}) collective-permute-start(bf16[3,32,256]{2,1,0:T(8,128)(2,1)S(1)} %get-tuple-element.63), channel_id=1, source_target_pairs={{2,4},{4,2},{6,8},{8,6},{10,12},{12,10},{14,0},{0,14},{3,5},{5,3},... | collective-permute-start | bytes 147464 | tf_op jit(solution)/shard_map/ppermute | solution.py:589
  28.3 5.2 %collective-permute-start.9 = (bf16[32,128]{1,0:T(8,128)(2,1)S(1)}, bf16[32,128]{1,0:T(8,128)(2,1)S(1)}, u32[]{:S(2)}, u32[]{:S(2)}) collective-permute-start(bf16[32,128]{1,0:T(8,128)(2,1)S(1)} %get-tuple-element.64), channel_id=1, source_target_pairs={{0,1},{1,0},{2,3},{3,2},{4,5},{5,4},{6,7},{7,6},{8,9},{9,8},{10,11... | collective-permute-start | bytes 24584 | tf_op jit(solution)/shard_map/ppermute | solution.py:590
  39.5 10.4 %collective-permute-start.10 = (bf16[3,32,256]{2,1,0:T(8,128)(2,1)S(1)}, bf16[3,32,256]{2,1,0:T(8,128)(2,1)S(1)}, u32[]{:S(2)}, u32[]{:S(2)}) collective-permute-start(bf16[3,32,256]{2,1,0:T(8,128)(2,1)S(1)} %get-tuple-element.66), channel_id=1, source_target_pairs={{0,16},{16,0},{32,48},{48,32},{64,80},{80,64},{96,112},{112,96},{1... | collective-permute-start | bytes 147464 | tf_op jit(solution)/shard_map/ppermute | solution.py:586
  39.6 10.3 %collective-permute-start.11 = (bf16[3,32,256]{2,1,0:T(8,128)(2,1)S(1)}, bf16[3,32,256]{2,1,0:T(8,128)(2,1)S(1)}, u32[]{:S(2)}, u32[]{:S(2)}) collective-permute-start(bf16[3,32,256]{2,1,0:T(8,128)(2,1)S(1)} %get-tuple-element.67), channel_id=1, source_target_pairs={{16,32},{32,16},{48,64},{64,48},{80,96},{96,80},{112,0},{0,112},{1... | collective-permute-start | bytes 147464 | tf_op jit(solution)/shard_map/ppermute | solution.py:587
  40.8 9.1 %collective-permute-start.12 = (bf16[3,32,256]{2,1,0:T(8,128)(2,1)S(1)}, bf16[3,32,256]{2,1,0:T(8,128)(2,1)S(1)}, u32[]{:S(2)}, u32[]{:S(2)}) collective-permute-start(bf16[3,32,256]{2,1,0:T(8,128)(2,1)S(1)} %get-tuple-element.68), channel_id=1, source_target_pairs={{0,2},{2,0},{4,6},{6,4},{8,10},{10,8},{12,14},{14,12},{1,3},{3,1},... | collective-permute-start | bytes 147464 | tf_op jit(solution)/shard_map/ppermute | solution.py:588
  41.4 8.5 %collective-permute-start.13 = (bf16[3,32,256]{2,1,0:T(8,128)(2,1)S(1)}, bf16[3,32,256]{2,1,0:T(8,128)(2,1)S(1)}, u32[]{:S(2)}, u32[]{:S(2)}) collective-permute-start(bf16[3,32,256]{2,1,0:T(8,128)(2,1)S(1)} %get-tuple-element.69), channel_id=1, source_target_pairs={{2,4},{4,2},{6,8},{8,6},{10,12},{12,10},{14,0},{0,14},{3,5},{5,3},... | collective-permute-start | bytes 147464 | tf_op jit(solution)/shard_map/ppermute | solution.py:589
  44.8 5.2 %collective-permute-start.14 = (bf16[32,128]{1,0:T(8,128)(2,1)S(1)}, bf16[32,128]{1,0:T(8,128)(2,1)S(1)}, u32[]{:S(2)}, u32[]{:S(2)}) collective-permute-start(bf16[32,128]{1,0:T(8,128)(2,1)S(1)} %get-tuple-element.70), channel_id=1, source_target_pairs={{0,1},{1,0},{2,3},{3,2},{4,5},{5,4},{6,7},{7,6},{8,9},{9,8},{10,11... | collective-permute-start | bytes 24584 | tf_op jit(solution)/shard_map/ppermute | solution.py:590
  56.0 12.4 %copy-start = (f32[3,2,1024,128]{3,2,1,0:T(8,128)}, f32[3,2,1024,128]{3,2,1,0:T(8,128)S(1)}, u32[]{:S(2)}) copy-start(f32[3,2,1024,128]{3,2,1,0:T(8,128)S(1)} %get-tuple-element.71.u) | copy-start | bytes 9437188
  56.0 8.2 %collective-permute-start.15 = (bf16[3,32,256]{2,1,0:T(8,128)(2,1)S(1)}, bf16[3,32,256]{2,1,0:T(8,128)(2,1)S(1)}, u32[]{:S(2)}, u32[]{:S(2)}) collective-permute-start(bf16[3,32,256]{2,1,0:T(8,128)(2,1)S(1)} %get-tuple-element.73), channel_id=1, source_target_pairs={{0,16},{16,0},{32,48},{48,32},{64,80},{80,64},{96,112},{112,96},{1... | collective-permute-start | bytes 147464 | tf_op jit(solution)/shard_map/ppermute | solution.py:586
  56.1 8.1 %collective-permute-start.16 = (bf16[3,32,256]{2,1,0:T(8,128)(2,1)S(1)}, bf16[3,32,256]{2,1,0:T(8,128)(2,1)S(1)}, u32[]{:S(2)}, u32[]{:S(2)}) collective-permute-start(bf16[3,32,256]{2,1,0:T(8,128)(2,1)S(1)} %get-tuple-element.74), channel_id=1, source_target_pairs={{16,32},{32,16},{48,64},{64,48},{80,96},{96,80},{112,0},{0,112},{1... | collective-permute-start | bytes 147464 | tf_op jit(solution)/shard_map/ppermute | solution.py:587
  57.0 7.2 %collective-permute-start.17 = (bf16[3,32,256]{2,1,0:T(8,128)(2,1)S(1)}, bf16[3,32,256]{2,1,0:T(8,128)(2,1)S(1)}, u32[]{:S(2)}, u32[]{:S(2)}) collective-permute-start(bf16[3,32,256]{2,1,0:T(8,128)(2,1)S(1)} %get-tuple-element.75), channel_id=1, source_target_pairs={{0,2},{2,0},{4,6},{6,4},{8,10},{10,8},{12,14},{14,12},{1,3},{3,1},... | collective-permute-start | bytes 147464 | tf_op jit(solution)/shard_map/ppermute | solution.py:588
  57.2 7.0 %collective-permute-start.18 = (bf16[3,32,256]{2,1,0:T(8,128)(2,1)S(1)}, bf16[3,32,256]{2,1,0:T(8,128)(2,1)S(1)}, u32[]{:S(2)}, u32[]{:S(2)}) collective-permute-start(bf16[3,32,256]{2,1,0:T(8,128)(2,1)S(1)} %get-tuple-element.76), channel_id=1, source_target_pairs={{2,4},{4,2},{6,8},{8,6},{10,12},{12,10},{14,0},{0,14},{3,5},{5,3},... | collective-permute-start | bytes 147464 | tf_op jit(solution)/shard_map/ppermute | solution.py:589
  59.0 5.2 %collective-permute-start.19 = (bf16[32,128]{1,0:T(8,128)(2,1)S(1)}, bf16[32,128]{1,0:T(8,128)(2,1)S(1)}, u32[]{:S(2)}, u32[]{:S(2)}) collective-permute-start(bf16[32,128]{1,0:T(8,128)(2,1)S(1)} %get-tuple-element.77), channel_id=1, source_target_pairs={{0,1},{1,0},{2,3},{3,2},{4,5},{5,4},{6,7},{7,6},{8,9},{9,8},{10,11... | collective-permute-start | bytes 24584 | tf_op jit(solution)/shard_map/ppermute | solution.py:590
  83.2 11.6 %all-to-all-start.1 = ((bf16[32,32,256]{2,1,0:T(8,128)(2,1)}), bf16[32,32,256]{2,1,0:T(8,128)(2,1)S(1)}, u32[]{:S(2)}, u32[]{:S(2)}) async-start(bf16[32,32,256]{2,1,0:T(8,128)(2,1)} %shard_map.102), calls=%async_computation.1 | async-start | bytes 1048576 | tf_op jit(solution)/shard_map/all_to_all | solution.py:666
  88.9 1.0 copy-start.2
  89.9 1.9 %copy-start.1 = (f32[3,2,1024,128]{3,2,1,0:T(8,128)S(1)}, f32[3,2,1024,128]{3,2,1,0:T(8,128)}, u32[]{:S(2)}) copy-start(f32[3,2,1024,128]{3,2,1,0:T(8,128)} %copy-done) | copy-start | bytes 9437188
  91.8 3.0 %copy-start.6 = (s32[8,16]{1,0:T(8,128)S(1)}, s32[8,16]{1,0:T(8,128)}, u32[]{:S(2)}) copy-start(s32[8,16]{1,0:T(8,128)} %counts.1) | copy-start | bytes 1540
  91.8 3.0 %copy-start.7 = (s32[1,8]{1,0:T(1,128)S(1)}, s32[1,8]{1,0:T(1,128)}, u32[]{:S(2)}) copy-start(s32[1,8]{1,0:T(1,128)} %listing.1) | copy-start | bytes 100
  94.8 1.2 %copy-start.3 = (f32[2,1024,128]{2,1,0:T(8,128)S(1)}, f32[2,1024,128]{2,1,0:T(8,128)}, u32[]{:S(2)}) copy-start(f32[2,1024,128]{2,1,0:T(8,128)} %copy-done.2) | copy-start | bytes 3145732

commit v2 on v1

v2 whole, which is shorter than its diff:
```python
import jax
import jax.numpy as jnp
from jax import lax
from jax.experimental import pallas as pl
from jax.experimental.pallas import tpu as pltpu
from jax.sharding import PartitionSpec as P

TILE = 32
SWEEPS = 4
RELAX = 0.6
ADVANCE = 0.5
PSEUDO = 0.3
CX, CY, CZ = 32, 32, 256
NY = 256
ROWS = CX * CY
LANES = 128
CHUNK = 8
UNROLL = 5
TINY = 1e-37
F32, BF16 = jnp.float32, jnp.bfloat16
LIMIT = 10 << 20


SWAP_NEAR = [(i, i ^ 1) for i in range(8)]
SWAP_FAR = [(1, 2), (2, 1), (3, 4), (4, 3), (5, 6), (6, 5), (7, 0), (0, 7)]
SWAP_Z = [(0, 1), (1, 0)]

VM = pl.BlockSpec(memory_space=pltpu.VMEM)
SM = pl.BlockSpec(memory_space=pltpu.SMEM)
ANY = pl.BlockSpec(memory_space=pltpu.HBM)
LOOSE = pl.BlockSpec(memory_space=pl.ANY)
CELLS = [(half, r) for r in range(4) for half in range(2)]
HALVES = (slice(0, LANES), slice(LANES, 2 * LANES))


def shape(*dims, dtype=F32):
    return jax.ShapeDtypeStruct(dims, dtype)


def call(kernel, outs, scratch, args, specs=None, out_specs=None):
    return pl.pallas_call(
        kernel,
        out_shape=outs,
        in_specs=specs or [VM] * len(args),
        out_specs=out_specs or [VM] * len(outs),
        scratch_shapes=scratch,
        compiler_params=pltpu.CompilerParams(vmem_limit_bytes=LIMIT),
    )(*args)


class Place:
    def __init__(self):
        gx, gy, ga = lax.axis_index("gx"), lax.axis_index("gy"), lax.axis_index("ga")
        self.even_x, self.even_y = gx % 2 == 0, gy % 2 == 0
        self.x_lo = (gx > 0).astype(F32)
        self.x_hi = (gx < lax.axis_size("gx") - 1).astype(F32)
        self.y_lo = (gy > 0).astype(F32)
        self.y_hi = (gy < lax.axis_size("gy") - 1).astype(F32)
        self.first_z = ga == 0
        self.z_hi = (ga == 0).astype(F32)
        self.z_lo = (ga != 0).astype(F32)


def rows(x):
    return pl.ds(pl.multiple_of(x * CY, CY), CY)


def load(ref, x, half, r, *lead):
    start = pl.multiple_of(x * CY + r * 8, 8)
    return ref[(*lead, half, pl.ds(start, 8), slice(None))]


def store(ref, x, half, r, value, *lead):
    start = pl.multiple_of(x * CY + r * 8, 8)
    ref[(*lead, half, pl.ds(start, 8), slice(None))] = value


def load_natural(ref, x, half, r, *lead):
    return ref[(*lead, half, x, pl.ds(r, 8, stride=4), slice(None))]


def store_natural(ref, x, half, r, value, *lead):
    ref[(*lead, half, x, pl.ds(r, 8, stride=4), slice(None))] = value


def small_iotas():
    sub = lax.broadcasted_iota(jnp.int32, (8, LANES), 0)
    lane = lax.broadcasted_iota(jnp.int32, (8, LANES), 1)
    return sub, lane


def y_sides(sub, r, get, low, high):
    below = get(r - 1) if r else jnp.where(sub == 0, low(), pltpu.roll(get(3), 1, 0))
    above = get(r + 1) if r < 3 else jnp.where(sub == 7, high(), pltpu.roll(get(0), 7, 0))
    return below, above


def z_sides(lane, tiles, low, high):
    down = [pltpu.roll(tile, 1, 1) for tile in tiles]
    up = [pltpu.roll(tile, LANES - 1, 1) for tile in tiles]
    below = [jnp.where(lane == 0, low, down[0]), jnp.where(lane == 0, down[0], down[1])]
    above = [
        jnp.where(lane == LANES - 1, up[1], up[0]),
        jnp.where(lane == LANES - 1, high, up[1]),
    ]
    return below, above


def column(place, zh, index):
    target = jnp.where(place.first_z, LANES - 1, 0)
    return pltpu.roll(zh, lax.rem(target - index + 256, LANES), 1)


STEP = CX + 1


def keep_rows(strips, c, x, half, r, value):
    if r == 0:
        strips[c, 0, half, pl.ds(x, 8, stride=STEP), :] = value
    if r == 3:
        strips[c, 1, half, pl.ds(x + 1, 8, stride=STEP), :] = value


def emit_faces(place, fields, strips, xs, ys):
    near_x = jnp.where(place.even_x, CX - 1, 0)
    last = 7 * STEP + 1
    for c, (ref, lead) in enumerate(fields):
        for half in range(2):
            for turn in range(2):
                x = near_x if turn == 0 else CX - 1 - near_x
                plane = ref[(*lead, half, rows(x), slice(None))]
                xs[turn][c, :, HALVES[half]] = plane.astype(BF16)
            low, high = strips[c, 0, half, 0:CX, :], strips[c, 1, half, last : last + CX, :]
            ys[0][c, :, HALVES[half]] = jnp.where(place.even_y, high, low).astype(BF16)
            ys[1][c, :, HALVES[half]] = jnp.where(place.even_y, low, high).astype(BF16)


def strip_scratch(count):
    return [pltpu.VMEM((count, 2, 2, 8 * STEP + 8, LANES), F32)]


class ZFace:
    def __init__(self, place):
        source = jnp.where(place.first_z, LANES - 1, 0)
        pick = lax.broadcasted_iota(jnp.int32, (LANES, LANES), 0) == source
        self.pick = jnp.where(pick, 1.0, 0.0).astype(BF16)
        self.lane = lax.broadcasted_iota(jnp.int32, (CY, LANES), 1)
        self.first_z = place.first_z

    def begin(self):
        return jnp.zeros((CY, LANES), F32)

    def add(self, total, x, edges):
        chosen = [
            jnp.where(self.first_z, high, low) for pairs in edges for low, high in pairs
        ]
        wide = jnp.concatenate(chosen, axis=0).astype(BF16)
        wide = jnp.dot(wide, self.pick, preferred_element_type=F32)
        for c in range(len(edges)):
            total = jnp.where(self.lane == c * CX + x, wide[c * CY : (c + 1) * CY], total)
        return total

    def whole(self, ref, group=8):
        edge = jnp.where(self.first_z, 1, 0)
        total = self.begin()
        for c in range(3):
            for block in range(CX // group):
                part = pl.ds(block * group * CY, group * CY)
                wide = ref[c, edge, part, :].astype(BF16)
                wide = jnp.dot(wide, self.pick, preferred_element_type=F32)
                for k in range(group):
                    hit = self.lane == c * CX + block * group + k
                    total = jnp.where(hit, wide[k * CY : (k + 1) * CY], total)
        return total


def stage_halos(place, rx, ry, xh, yh, count):
    for c in range(count):
        near, far = rx[0][c].astype(F32), rx[1][c].astype(F32)
        xh[0, c] = jnp.where(place.even_x, far, near)
        xh[1, c] = jnp.where(place.even_x, near, far)
        near, far = ry[0][c].astype(F32), ry[1][c].astype(F32)
        low, high = jnp.where(place.even_y, far, near), jnp.where(place.even_y, near, far)
        for h, half in enumerate(HALVES):
            yh[0, c, h] = low[:, half]
            yh[1, c, h] = high[:, half]


def over_planes(step, end, within):
    step(0, lambda *at: end(0, *at), lambda *at: within(1, *at))

    def inner(block, carry):
        for k in range(UNROLL):
            x = 1 + block * UNROLL + k
            step(x, lambda *at: within(x - 1, *at), lambda *at: within(x + 1, *at))
        return carry

    lax.fori_loop(0, (CX - 2) // UNROLL, inner, 0)
    step(CX - 1, lambda *at: within(CX - 2, *at), lambda *at: end(1, *at))


def halo_plane(xh, side, c, half, r):
    return xh[side, c, r * 8 : r * 8 + 8, HALVES[half]]


def pack_kernel(
    prev, level, support, u0, lev, free, xs1, xs2, ys1, ys2, zs, prev_in, level_in, support_in, sems,
    strips,
):
    place = Place()
    copies = []
    for i in range(CX // CHUNK):
        part, trio = pl.ds(i * CHUNK, CHUNK), []
        for h, half in enumerate(HALVES):
            pairs = [(prev.at[c, part, :, half], prev_in.at[c, h, part]) for c in range(3)]
            pairs.append((level.at[part, :, half], level_in.at[h, part]))
            pairs.append((support.at[part, :, half], support_in.at[h, part]))
            for source, target in pairs:
                sem = sems.at[i, len(trio)]
                trio.append(pltpu.make_async_copy(source, target, sem))
        copies.append(trio)
    for trio in copies:
        for one in trio:
            one.start()
    face = ZFace(place)
    total = face.begin()
    for i, trio in enumerate(copies):
        for one in trio:
            one.wait()

        def step(block, total):
            for k in range(4):
                x = i * CHUNK + block * 4 + k
                edges = [[], [], [], []]
                for r in range(4):
                    rows_of = [[], [], [], []]
                    for half in range(2):
                        keep = (1 - load_natural(support_in, x, half, r)).astype(F32)
                        store(free, x, half, r, keep)
                        for c in range(3):
                            value = load_natural(prev_in, x, half, r, c) * keep
                            store(u0, x, half, r, value, c)
                            keep_rows(strips, c, x, half, r, value)
                            rows_of[c].append(value)
                        value = load_natural(level_in, x, half, r)
                        store(lev, x, half, r, value)
                        keep_rows(strips, 3, x, half, r, value)
                        rows_of[3].append(value)
                    for c in range(4):
                        edges[c].append(rows_of[c])
                total = face.add(total, x, edges)
            return total

        total = lax.fori_loop(0, CHUNK // 4, step, total)
    fields = [(u0, (c,)) for c in range(3)] + [(lev, ())]
    emit_faces(place, fields, strips, (xs1, xs2), (ys1, ys2))
    zs[...] = total.astype(BF16)


def prepare_kernel(lev, load_mask, extension, tanh, loaded, turned, load_in, sem):
    copies = [
        pltpu.make_async_copy(load_mask.at[:, :, half], load_in.at[h], sem.at[h])
        for h, half in enumerate(HALVES)
    ]
    for one in copies:
        one.start()

    def bend(block, carry):
        for k in range(2):
            for half, r in CELLS:
                x = block * 2 + k
                store(tanh, x, half, r, jnp.tanh(load(lev, x, half, r)))
        return carry

    lax.fori_loop(0, CX // 2, bend, 0)
    for one in copies:
        one.wait()

    def turn(block, carry):
        for k in range(2):
            x = block * 2 + k
            for half, r in CELLS:
                store(loaded, x, half, r, load_natural(load_in, x, half, r).astype(F32))
        return carry

    lax.fori_loop(0, CX // 2, turn, 0)

    def order(size, along):
        place = lax.broadcasted_iota(jnp.int32, (size, size), along)
        other = lax.broadcasted_iota(jnp.int32, (size, size), 1 - along)
        source = place // CY * CY + place % 8 * 4 + place // 8 % 4
        return (source == other).astype(BF16)

    held = jnp.dot(order(CY, 0), extension[...], preferred_element_type=F32).astype(BF16)
    held = jnp.dot(held, order(NY, 1), preferred_element_type=F32)
    turned[...] = held.astype(BF16)


def sum_sides(place, sub, lane, x, r, u, yh, sides, x_below, x_above, weights):
    found = []
    for c in range(3):
        tiles = [load(u, x, half, r, c) for half in range(2)]
        side = sides[c][r * 8 : r * 8 + 8]
        z_below, z_above = z_sides(lane, tiles, side, side)
        sums = []
        for half in range(2):
            xl, xu, yl, yu, zl, zu = (weight[half] for weight in weights)
            y_below, y_above = y_sides(
                sub,
                r,
                lambda row: load(u, x, half, row, c),
                lambda: yh[0, c, half, pl.ds(x, 8, stride=0), :],
                lambda: yh[1, c, half, pl.ds(x, 8, stride=0), :],
            )
            total = xl * x_below(c, half, r) + xu * x_above(c, half, r)
            total = total + (yl * y_below + yu * y_above)
            total = total + (zl * z_below[half] + zu * z_above[half])
            sums.append(total)
        found.append((tiles, sums))
    return found


def columns(place, zh, x):
    return [column(place, zh, c * CX + x) for c in range(3)]


def stored_weights(x, r, wx, wyl, wyh, wzl, wzh):
    pairs = [(wx, x), (wx, x + 1), (wyl, x), (wyh, x), (wzl, x), (wzh, x)]
    return [[load(ref, at, half, r) for half in range(2)] for ref, at in pairs]


def first_kernel(
    traction, u, lev, free, tanh, loaded, rx1, rx2, ry1, ry2, rz,
    new, xs1, xs2, ys1, ys2, zs, wx, wyl, wyh, wzl, wzh, coup, diag, gain, keep, push,
    xh, yh, zh, strips,
):
    place = Place()
    sub, lane = small_iotas()
    stage_halos(place, (rx1, rx2), (ry1, ry2), xh, yh, 4)
    zh[0] = rz[...].astype(F32)
    bent = jnp.tanh(zh[0])
    zh[1] = bent * place.z_lo
    zh[2] = bent * place.z_hi
    yh[0, 3] = jnp.tanh(yh[0, 3]) * place.y_lo
    yh[1, 3] = jnp.tanh(yh[1, 3]) * place.y_hi
    xh[0, 3] = jnp.tanh(xh[0, 3]) * place.x_lo
    xh[1, 3] = jnp.tanh(xh[1, 3]) * place.x_hi
    y_low = jnp.where(sub == 0, place.y_lo, 1.0)
    y_high = jnp.where(sub == 7, place.y_hi, 1.0)
    z_low = jnp.where(lane == 0, place.z_lo, 1.0)
    z_high = jnp.where(lane == LANES - 1, place.z_hi, 1.0)

    def weight(a, b):
        return 0.525 + 0.2375 * (a + b)

    def step(x, x_below, x_above):
        low_side, high_side = column(place, zh[1], 96 + x), column(place, zh[2], 96 + x)
        sides = columns(place, zh[0], x)
        for r in range(4):
            part = slice(r * 8, r * 8 + 8)
            centre = [load(tanh, x, half, r) for half in range(2)]
            z_below, z_above = z_sides(lane, centre, low_side[part], high_side[part])
            kept, cells = [[], [], [], [], [], []], []
            for half in range(2):
                mid = centre[half]
                y_below, y_above = y_sides(
                    sub,
                    r,
                    lambda row: load(tanh, x, half, row),
                    lambda: yh[0, 3, half, pl.ds(x, 8, stride=0), :],
                    lambda: yh[1, 3, half, pl.ds(x, 8, stride=0), :],
                )
                xl, xu = weight(mid, x_below(3, half, r)), weight(mid, x_above(3, half, r))
                yl, yu = weight(mid, y_below), weight(mid, y_above)
                zl, zu = weight(mid, z_below[half]), weight(mid, z_above[half])
                total = (xl + xu) + (yl + yu) + (zl + zu)
                middle = 0.2625 + 0.2375 * mid
                factor = RELAX * load(free, x, half, r) / (total + middle)
                stay, force = 1.0 - factor * total, factor * load(loaded, x, half, r)
                if r == 0:
                    yl = yl * y_low
                if r == 3:
                    yu = yu * y_high
                if half == 0:
                    zl = zl * z_low
                else:
                    zu = zu * z_high
                if isinstance(x, int) and x == 0:
                    xl = xl * place.x_lo
                    store(wx, 0, half, r, xl)
                if isinstance(x, int) and x == CX - 1:
                    xu = xu * place.x_hi
                store(wx, x + 1, half, r, xu)
                stored = (wyl, yl), (wyh, yu), (wzl, zl), (wzh, zu), (coup, middle)
                stored += (diag, total), (gain, factor), (keep, stay), (push, force)
                for ref, value in stored:
                    store(ref, x, half, r, value)
                for into, one in zip(kept, (xl, xu, yl, yu, zl, zu)):
                    into.append(one)
                cells.append((middle, factor, stay, force))
            found = sum_sides(
                place, sub, lane, x, r, u, yh, sides, x_below, x_above, kept
            )
            update(traction, found, cells, x, r, new, strips)

    def end(side, c, half, r):
        return halo_plane(xh, side, c, half, r)

    def within(x, c, half, r):
        return load(tanh, x, half, r) if c == 3 else load(u, x, half, r, c)

    over_planes(step, end, within)
    emit_faces(place, [(new, (c,)) for c in range(3)], strips, (xs1, xs2), (ys1, ys2))
    zs[...] = ZFace(place).whole(new).astype(BF16)


def update(traction, found, cells, x, r, new, strips):
    for half in range(2):
        middle, factor, stay, force = cells[half]
        shared = middle * (found[0][0][half] + found[1][0][half] + found[2][0][half])
        for c in range(3):
            tile, near = found[c][0][half], found[c][1][half]
            value = stay * tile + factor * (near - shared) + traction[c] * force
            store(new, x, half, r, value, c)
            keep_rows(strips, c, x, half, r, value)


def sweep_kernel(
    traction, u, wx, wyl, wyh, wzl, wzh, coup, diag, gain, keep, push, rx1, rx2, ry1, ry2, rz, held,
    new, xs1, xs2, ys1, ys2, zs, xh, yh, zh, strips,
):
    place = Place()
    sub, lane = small_iotas()
    stage_halos(place, (rx1, rx2), (ry1, ry2), xh, yh, 3)
    zh[...] = rz[...].astype(F32)

    def step(x, x_below, x_above):
        sides = columns(place, zh[...], x)
        for r in range(4):
            weights = stored_weights(x, r, wx, wyl, wyh, wzl, wzh)
            cells = [
                [load(ref, x, half, r) for ref in (coup, gain, keep, push)] for half in range(2)
            ]
            found = sum_sides(
                place, sub, lane, x, r, u, yh, sides, x_below, x_above, weights
            )
            update(traction, found, cells, x, r, new, strips)

    over_planes(
        step,
        lambda side, c, half, r: halo_plane(xh, side, c, half, r),
        lambda x, c, half, r: load(u, x, half, r, c),
    )
    emit_faces(place, [(new, (c,)) for c in range(3)], strips, (xs1, xs2), (ys1, ys2))
    zs[...] = ZFace(place).whole(new).astype(BF16)


def energy_kernel(
    u, tanh, wx, wyl, wyh, wzl, wzh, coup, diag, extension, rx1, rx2, ry1, ry2, rz, held,
    out, xh, yh, zh,
):
    place = Place()
    sub, lane = small_iotas()
    stage_halos(place, (rx1, rx2), (ry1, ry2), xh, yh, 3)
    zh[...] = rz[...].astype(F32)

    def step(x, x_below, x_above):
        sides = columns(place, zh[...], x)
        values = [[], []]
        for r in range(4):
            weights = stored_weights(x, r, wx, wyl, wyh, wzl, wzh)
            found = sum_sides(
                place, sub, lane, x, r, u, yh, sides, x_below, x_above, weights
            )
            for half in range(2):
                shared = found[0][0][half] + found[1][0][half] + found[2][0][half]
                shared = load(coup, x, half, r) * shared
                total = load(diag, x, half, r)
                energy = None
                for c in range(3):
                    tile, near = found[c][0][half], found[c][1][half]
                    term = tile * (total * tile + shared - near)
                    energy = term if energy is None else energy + term
                bent = load(tanh, x, half, r)
                values[half].append((0.5 - 0.5 * bent * bent) * energy)
        for half in range(2):
            whole = jnp.concatenate(values[half], axis=0)
            out[x + x // 4, :, HALVES[half]] = whole.astype(BF16)

    over_planes(
        step,
        lambda side, c, half, r: halo_plane(xh, side, c, half, r),
        lambda x, c, half, r: load(u, x, half, r, c),
    )
    for part in range(8):
        out[5 * part + 4] = extension[...]


def unpack_kernel(u, out, token, natural, sems):
    copies = []
    token[...] = jnp.zeros_like(token)
    for c in range(3):

        def step(block, carry):
            for k in range(2):
                x = block * 2 + k
                for half, r in CELLS:
                    store_natural(natural, x, half, r, load(u, x, half, r, c), c)
            return carry

        lax.fori_loop(0, CX // 2, step, 0)
        for h, half in enumerate(HALVES):
            one = pltpu.make_async_copy(natural.at[c, h], out.at[c, :, :, half], sems.at[c, h])
            one.start()
            copies.append(one)
    for one in copies:
        one.wait()


def product_kernel(received, out):
    matrix = jnp.concatenate([received[5 * part + 4] for part in range(8)], axis=0)
    for x in range(4):
        field = jnp.concatenate([received[5 * part + x] for part in range(8)], axis=0)
        moved = jnp.dot(matrix, field, preferred_element_type=F32).astype(BF16)
        for part in range(8):
            out[4 * part + x] = moved[CY * part : CY * (part + 1)]


def slopes_kernel(lev, rx1, rx2, ry1, ry2, rz, grow, shrink, xh, yh, zh):
    place = Place()
    sub, lane = small_iotas()
    near, far = rx1[3].astype(F32), rx2[3].astype(F32)
    xh[0] = jnp.where(place.even_x, far, near) * place.x_lo
    xh[1] = jnp.where(place.even_x, near, far) * place.x_hi
    near, far = ry1[3].astype(F32), ry2[3].astype(F32)
    low = jnp.where(place.even_y, far, near) * place.y_lo
    high = jnp.where(place.even_y, near, far) * place.y_hi
    for h, half in enumerate(HALVES):
        yh[0, h] = low[:, half]
        yh[1, h] = high[:, half]
    zh[0] = rz[...].astype(F32) * place.z_lo
    zh[1] = rz[...].astype(F32) * place.z_hi

    def root(total):
        return total * lax.rsqrt(jnp.maximum(total, TINY))

    def step(x, x_below, x_above):
        low_side, high_side = column(place, zh[0], 96 + x), column(place, zh[1], 96 + x)
        for r in range(4):
            part = slice(r * 8, r * 8 + 8)
            centre = [load(lev, x, half, r) for half in range(2)]
            z_below, z_above = z_sides(lane, centre, low_side[part], high_side[part])
            for half in range(2):
                mid = centre[half]
                y_pair = y_sides(
                    sub,
                    r,
                    lambda row: load(lev, x, half, row),
                    lambda: yh[0, half, pl.ds(x, 8, stride=0), :],
                    lambda: yh[1, half, pl.ds(x, 8, stride=0), :],
                )
                growing, shrinking = 0.0, 0.0
                x_pair = (x_below(half, r), x_above(half, r))
                for below, above in (x_pair, y_pair, (z_below[half], z_above[half])):
                    up = jnp.maximum(mid - jnp.minimum(below, above), 0.0)
                    down = jnp.maximum(jnp.maximum(below, above) - mid, 0.0)
                    growing = growing + up * up
                    shrinking = shrinking + down * down
                store(grow, x, half, r, ADVANCE * root(growing))
                store(shrink, x, half, r, ADVANCE * root(shrinking))

    over_planes(
        step,
        lambda side, half, r: xh[side, r * 8 : r * 8 + 8, HALVES[half]],
        lambda x, half, r: load(lev, x, half, r),
    )


def final_kernel(
    counts, listing, lev, velocity, grow, shrink, out, first, second, sign, ways, natural, sems
):
    gx, gy, ga = lax.axis_index("gx"), lax.axis_index("gy"), lax.axis_index("ga")
    sub, lane = small_iotas()
    own = counts[gx, gy * lax.axis_size("ga") + ga]
    listed = []
    for half in range(2):
        tile = lane // TILE + half * (LANES // TILE)
        mask = jnp.zeros((8, LANES), F32)
        for entry in range(CZ // TILE):
            hit = jnp.where(entry < own, listing[0, entry], -1)
            mask = jnp.where(tile == hit, PSEUDO, mask)
        listed.append(mask)
    low_z, high_z = lane % TILE == 0, lane % TILE == TILE - 1

    def advance(block, carry):
        for k in range(4):
            x = block * 4 + k
            for half in range(2):
                plane = velocity[x, :, HALVES[half]].astype(F32)
                for r in range(4):
                    moved = plane[r * 8 : r * 8 + 8]
                    speed = moved / (1.0 + jnp.abs(moved))
                    ahead = jnp.where(moved > 0.0, load(grow, x, half, r), load(shrink, x, half, r))
                    value = load(lev, x, half, r) - speed * ahead
                    store(first, x, half, r, value)
                    store(sign, x, half, r, listed[half] * (value * lax.rsqrt(value * value + 1.0)))
                    store(ways, x, half, r, jnp.where(value > 0.0, 1.0, -1.0))
        return carry

    lax.fori_loop(0, CX // 4, advance, 0)

    def sweep(source, x, half, r):
        centre = load(source, x, half, r)
        strength = load(sign, x, half, r)
        way = load(ways, x, half, r)
        sides = (
            (
                load(source, jnp.maximum(x - 1, 0), half, r),
                load(source, jnp.minimum(x + 1, CX - 1), half, r),
            ),
            y_sides(
                sub, r, lambda row: load(source, x, half, row), lambda: centre, lambda: centre
            ),
            (
                jnp.where(low_z, centre, pltpu.roll(centre, 1, 1)),
                jnp.where(high_z, centre, pltpu.roll(centre, LANES - 1, 1)),
            ),
        )
        faced = way * centre
        total = None
        for below, above in sides:
            rise = jnp.maximum(faced - jnp.minimum(way * below, way * above), 0.0)
            total = rise * rise if total is None else total + rise * rise
        root = total * lax.rsqrt(jnp.maximum(total, TINY))
        return centre - strength * (root - 1.0)

    buffers = [first, second]
    for turn in range(SWEEPS - 1):
        source, target = buffers[turn % 2], buffers[(turn + 1) % 2]

        def step(block, carry):
            for k in range(4):
                x = block * 4 + k
                for half, r in CELLS:
                    store(target, x, half, r, sweep(source, x, half, r))
            return carry

        lax.fori_loop(0, CX // 4, step, 0)
    source = buffers[(SWEEPS - 1) % 2]
    copies = []
    for i in range(CX // CHUNK):

        def last(block, carry):
            for k in range(4):
                x = i * CHUNK + block * 4 + k
                for half, r in CELLS:
                    store_natural(natural, x, half, r, sweep(source, x, half, r))
            return carry

        lax.fori_loop(0, CHUNK // 4, last, 0)
        part = pl.ds(i * CHUNK, CHUNK)
        for h, half in enumerate(HALVES):
            one = pltpu.make_async_copy(natural.at[h, part], out.at[part, :, half], sems.at[i, h])
            one.start()
            copies.append(one)
    for one in copies:
        one.wait()


def exchange(xs1, xs2, ys1, ys2, zs):
    return (
        lax.ppermute(xs1, "gx", SWAP_NEAR),
        lax.ppermute(xs2, "gx", SWAP_FAR),
        lax.ppermute(ys1, "gy", SWAP_NEAR),
        lax.ppermute(ys2, "gy", SWAP_FAR),
        lax.ppermute(zs, "ga", SWAP_Z),
    )


def faces(count):
    return [shape(count, 32, CZ, dtype=BF16)] * 4 + [shape(CY, LANES, dtype=BF16)]


def halo_scratch(count):
    return [pltpu.VMEM((2, count, CY, CZ), F32), pltpu.VMEM((2, count, 2, CX, LANES), F32)]


def local(
    level_set, displacement_prev, traction, load_mask, support_mask, extension, tile_count, tile_list
):
    displacement_prev, level_set, support_mask, load_mask = (
        pltpu.with_memory_space_constraint(x, pltpu.HBM)
        for x in (displacement_prev, level_set, support_mask, load_mask)
    )
    flat = shape(2, ROWS, LANES)
    field = shape(3, 2, ROWS, LANES)
    column_scratch = pltpu.VMEM((CY, LANES), F32)
    u, lev, free, *sent = call(
        pack_kernel,
        [field, flat, flat] + faces(4),
        [
            pltpu.VMEM((3, 2, CX, CY, LANES), F32),
            pltpu.VMEM((2, CX, CY, LANES), F32),
            pltpu.VMEM((2, CX, CY, LANES), jnp.int32),
            pltpu.SemaphoreType.DMA((CX // CHUNK, 10)),
        ]
        + strip_scratch(4),
        (displacement_prev, level_set, support_mask),
        [ANY] * 3,
    )
    got = exchange(*sent)
    level_got = got
    tanh, loaded, turned = call(
        prepare_kernel,
        [flat] * 2 + [shape(CY, NY, dtype=BF16)],
        [pltpu.VMEM((2, CX, CY, LANES), jnp.int32), pltpu.SemaphoreType.DMA((2,))],
        (lev, load_mask, extension),
        [VM, ANY, VM],
    )
    u, *rest = call(
        first_kernel,
        [field] + faces(3) + [shape(2, ROWS + CY, LANES)] + [flat] * 9,
        halo_scratch(4) + [pltpu.VMEM((3, CY, LANES), F32)] + strip_scratch(3),
        (traction, u, lev, free, tanh, loaded, *got),
        [SM] + [VM] * 10,
    )
    sent, made = rest[:5], rest[5:]
    got = exchange(*sent)
    grow, shrink = call(
        slopes_kernel, [flat] * 2,
        [pltpu.VMEM((2, CY, CZ), F32), pltpu.VMEM((2, 2, CX, LANES), F32)]
        + [pltpu.VMEM((2, CY, LANES), F32)],
        (lev, *level_got),
    )
    for turn in range(2):
        u, *sent = call(
            sweep_kernel, [field] + faces(3),
            halo_scratch(3) + [column_scratch] + strip_scratch(3),
            (traction, u, *made, *got, grow),
            [SM] + [VM] * (len(made) + 6) + [LOOSE],
        )
        got = exchange(*sent)
    displacement, token = call(
        unpack_kernel, [shape(3, CX, CY, CZ), shape(8, LANES)],
        [pltpu.VMEM((3, 2, CX, CY, LANES), F32), pltpu.SemaphoreType.DMA((3, 2))],
        (u,), None, [ANY, VM],
    )
    (sensitivity,) = call(
        energy_kernel, [shape(40, CY, CZ, dtype=BF16)], halo_scratch(3) + [column_scratch],
        (u, tanh, *made[:7], turned, *got, token),
    )
    sensitivity = lax.all_to_all(sensitivity, "gy", split_axis=0, concat_axis=0, tiled=True)
    (velocity,) = call(product_kernel, [shape(CX, CY, CZ, dtype=BF16)], [], (sensitivity,))
    velocity = lax.all_to_all(velocity, "gy", split_axis=0, concat_axis=0, tiled=True)
    (level_new,) = call(
        final_kernel, [shape(CX, CY, CZ)],
        [pltpu.VMEM((2, ROWS, LANES), F32)] * 4
        + [pltpu.VMEM((2, CX, CY, LANES), F32), pltpu.SemaphoreType.DMA((CX // CHUNK, 2))],
        (tile_count, tile_list, lev, velocity, grow, shrink),
        [SM, SM] + [VM] * 4,
        [ANY],
    )
    return (displacement, level_new)


def solution(mesh):
    return jax.shard_map(
        local,
        mesh=mesh,
        in_specs=(
            P("gx", "gy", "ga"),
            P(None, "gx", "gy", "ga"),
            P(),
            P("gx", "gy", "ga"),
            P("gx", "gy", "ga"),
            P("gy", None),
            P(),
            P(("gx", "gy", "ga"), None),
        ),
        out_specs=(P(None, "gx", "gy", "ga"), P("gx", "gy", "ga")),
        check_vma=False,
    )
```

time: 107 us -> 93.4 us (0.87)
  Pallas kernels: 44.4 us -> 32.5 us
  blocking collectives: 13.7 us -> 24.8 us
  waiting for transfers between devices: 9.88 us -> 5.22 us
  local copies, waits for them, and re-layouts: 4.1 us -> 0.02 us
  starting transfers between devices: 33.3 us -> 29.8 us
    pallas_call x10, Pallas kernels: 44.4 us -> 32.5 us  [call(): pl.pallas_call(kernel, out_shape=outs, in_specs=specs or [VM] * len(args)...]
    all_to_all x0 -> x1, blocking collectives: none -> 11 us  [local(): lax.all_to_all(velocity, 'gy', split_axis=0, concat_axis=0, tiled=True)]
    unnamed x16 -> x8, local copies, waits for them, and re-layouts: 4.1 us -> 0.02 us
    ppermute x4, waiting for transfers between devices: 8.75 us -> 5.18 us  [exchange(): lax.ppermute(zs, 'ga', SWAP_Z)]
    all_to_all x1 -> x0, starting transfers between devices: 3.49 us -> none  [local(): lax.all_to_all(velocity, 'gy', split_axis=0, concat_axis=0, tiled=True)]
    all_to_all x1 -> x0, waiting for transfers between devices: 1.1 us -> none  [local(): lax.all_to_all(velocity, 'gy', split_axis=0, concat_axis=0, tiled=True)]
  transfers between devices with their start and end apart: 21 -> 20, of which waited for: 4 -> 2; matrix products, arithmetic and copies ran while one was open for 0% -> 0% of each run, Pallas kernels for 5% -> 5%
where the time goes in v2:
time: 93.4 us; the launch traced here: 93.2 us
  Pallas kernels  32.5 us (35%)
  starting transfers between devices  29.8 us (32%)
  blocking collectives  24.8 us (27%)
  waiting for transfers between devices  5.22 us (6%)
    pallas_call x10, Pallas kernels, call(): pl.pallas_call(kernel, out_shape=outs, in_specs=specs or [VM] * len(args)...  32.5 us
    all_to_all x1, blocking collectives, local(): lax.all_to_all(sensitivity, 'gy', split_axis=0, concat_axis=0, tiled=True)  13.7 us
    all_to_all x1, blocking collectives, local(): lax.all_to_all(velocity, 'gy', split_axis=0, concat_axis=0, tiled=True)  11 us
    ppermute x4, starting transfers between devices, exchange(): lax.ppermute(zs, 'ga', SWAP_Z)  10.6 us
    ppermute x4, starting transfers between devices, exchange(): lax.ppermute(ys2, 'gy', SWAP_FAR)  9.97 us
    ppermute x4, starting transfers between devices, exchange(): lax.ppermute(xs2, 'gx', SWAP_FAR)  6.19 us
    ppermute x4, waiting for transfers between devices, exchange(): lax.ppermute(zs, 'ga', SWAP_Z)  5.18 us
    ppermute x4, starting transfers between devices, exchange(): lax.ppermute(ys1, 'gy', SWAP_NEAR)  2.69 us
  transfers between devices with their start and end apart: 20, of which 2 were waited for; matrix products, arithmetic and copies ran while one was open for 0% of the time, Pallas kernels for 5%

profile of v2, /device:TPU:0, one launch (start us, length us, event | category | flops | bytes accessed | tf_op | source)
XLA Modules:
  0.0 93.2 jit_solution(11994785122440865896)
XLA Ops:
  0.6 0.0 copy-start
  0.6 0.0 copy-start.1
  0.7 3.4 %shard_map.95 = (f32[3,2,1024,128]{3,2,1,0:T(8,128)S(1)}, f32[2,1024,128]{2,1,0:T(8,128)S(1)}, f32[2,1024,128]{2,1,0:T(8,128)S(1)}, bf16[4,32,256]{2,1,0:T(8,128...) custom-call(f32[3,32,32,256]{3,2,1,0:T(8,128)} %prev.1, ...), custom_call_target="tpu_custom_call" | custom-call | tf_op jit(solution)/shard_map/pallas_call | solution.py:41
  4.0 0.1 collective-permute-start
  4.1 3.0 %collective-permute-start.1 = (bf16[4,32,256]{2,1,0:T(8,128)(2,1)S(1)}, bf16[4,32,256]{2,1,0:T(8,128)(2,1)S(1)}, u32[]{:S(2)}, u32[]{:S(2)}) collective-permute-start(bf16[4,32,256]{2,1,0:T(8,128)(2,1)S(1)} %get-tuple-element.51), channel_id=1, source_target_pairs={{16,32},{32,16},{48,64},{64,48},{80,96},{96,80},{112,0},{0,112},{1... | collective-permute-start | bytes 196616 | tf_op jit(solution)/shard_map/ppermute | solution.py:673
  7.1 1.9 %collective-permute-start.2 = (bf16[4,32,256]{2,1,0:T(8,128)(2,1)S(1)}, bf16[4,32,256]{2,1,0:T(8,128)(2,1)S(1)}, u32[]{:S(2)}, u32[]{:S(2)}) collective-permute-start(bf16[4,32,256]{2,1,0:T(8,128)(2,1)S(1)} %get-tuple-element.52), channel_id=1, source_target_pairs={{0,2},{2,0},{4,6},{6,4},{8,10},{10,8},{12,14},{14,12},{1,3},{3,1},... | collective-permute-start | bytes 196616 | tf_op jit(solution)/shard_map/ppermute | solution.py:674
  9.0 2.6 %collective-permute-start.3 = (bf16[4,32,256]{2,1,0:T(8,128)(2,1)S(1)}, bf16[4,32,256]{2,1,0:T(8,128)(2,1)S(1)}, u32[]{:S(2)}, u32[]{:S(2)}) collective-permute-start(bf16[4,32,256]{2,1,0:T(8,128)(2,1)S(1)} %get-tuple-element.53), channel_id=1, source_target_pairs={{2,4},{4,2},{6,8},{8,6},{10,12},{12,10},{14,0},{0,14},{3,5},{5,3},... | collective-permute-start | bytes 196616 | tf_op jit(solution)/shard_map/ppermute | solution.py:675
  11.6 3.9 %collective-permute-start.4 = (bf16[32,128]{1,0:T(8,128)(2,1)S(1)}, bf16[32,128]{1,0:T(8,128)(2,1)S(1)}, u32[]{:S(2)}, u32[]{:S(2)}) collective-permute-start(bf16[32,128]{1,0:T(8,128)(2,1)S(1)} %get-tuple-element.54), channel_id=1, source_target_pairs={{0,1},{1,0},{2,3},{3,2},{4,5},{5,4},{6,7},{7,6},{8,9},{9,8},{10,11... | collective-permute-start | bytes 24584 | tf_op jit(solution)/shard_map/ppermute | solution.py:676
  15.5 0.0 copy-done
  15.5 1.6 %shard_map.96 = (f32[2,1024,128]{2,1,0:T(8,128)S(1)}, f32[2,1024,128]{2,1,0:T(8,128)S(1)}, bf16[32,256]{1,0:T(8,128)(2,1)S(1)}) custom-call(f32[2,1024,128]{2,1,0:T(8,128)S(1)} %get-tuple-element.46.lev, s32[32,32,256]{2,1,0:T(8,128)} %load_mask.1, bf16[32,256]{1,0:T(8,128)(2,1)S(1)} %copy-done), custom_call_target="tpu_custom_call" | custom-call | tf_op jit(solution)/shard_map/pallas_call | solution.py:41
  17.1 0.0 collective-permute-done.4.rz
  17.1 0.0 collective-permute-done.rx1
  17.1 0.0 collective-permute-done.1.rx2
  17.1 0.0 collective-permute-done.2.ry1
  17.1 0.0 collective-permute-done.3.ry2
  17.1 0.0 copy-done.1
  17.1 5.2 %shard_map.97 = (f32[3,2,1024,128]{3,2,1,0:T(8,128)S(1)}, bf16[3,32,256]{2,1,0:T(8,128)(2,1)S(1)}, bf16[3,32,256]{2,1,0:T(8,128)(2,1)S(1)}, bf16[3,32,256]{2,1,0...) custom-call(f32[3]{0:T(128)S(1)} %copy-done.1, ...), custom_call_target="tpu_custom_call" | custom-call | tf_op jit(solution)/shard_map/pallas_call | solution.py:41
  22.4 0.1 collective-permute-start.5
  22.5 0.9 collective-permute-start.6
  23.4 0.1 collective-permute-start.7
  23.5 2.2 %collective-permute-start.8 = (bf16[3,32,256]{2,1,0:T(8,128)(2,1)S(1)}, bf16[3,32,256]{2,1,0:T(8,128)(2,1)S(1)}, u32[]{:S(2)}, u32[]{:S(2)}) collective-permute-start(bf16[3,32,256]{2,1,0:T(8,128)(2,1)S(1)} %get-tuple-element.69), channel_id=1, source_target_pairs={{2,4},{4,2},{6,8},{8,6},{10,12},{12,10},{14,0},{0,14},{3,5},{5,3},... | collective-permute-start | bytes 147464 | tf_op jit(solution)/shard_map/ppermute | solution.py:675
  25.7 3.4 %collective-permute-start.9 = (bf16[32,128]{1,0:T(8,128)(2,1)S(1)}, bf16[32,128]{1,0:T(8,128)(2,1)S(1)}, u32[]{:S(2)}, u32[]{:S(2)}) collective-permute-start(bf16[32,128]{1,0:T(8,128)(2,1)S(1)} %get-tuple-element.70), channel_id=1, source_target_pairs={{0,1},{1,0},{2,3},{3,2},{4,5},{5,4},{6,7},{7,6},{8,9},{9,8},{10,11... | collective-permute-start | bytes 24584 | tf_op jit(solution)/shard_map/ppermute | solution.py:676
  29.1 1.7 %shard_map.98 = (f32[2,1024,128]{2,1,0:T(8,128)S(1)}, f32[2,1024,128]{2,1,0:T(8,128)S(1)}) custom-call(f32[2,1024,128]{2,1,0:T(8,128)S(1)} %get-tuple-element.46.lev, bf16[4,32,256]{2,1,0:T(8,128)(2,1)S(1)} %collective-permute-done.rx1, bf16[4,32,256]{2,1,0:T(8,128)(2,1)S(1)} %collective-permute-done.1.rx2, ...), custom_call_target="tpu_custom_call" | custom-call | tf_op jit(solution)/shard_map/pallas_call | solution.py:41
  30.8 0.0 collective-permute-done.9.rz
  30.9 0.0 collective-permute-done.5.rx1
  30.9 0.0 collective-permute-done.6.rx2
  30.9 0.0 collective-permute-done.7.ry1
  30.9 0.0 collective-permute-done.8.ry2
  30.9 4.1 %shard_map.99 = (f32[3,2,1024,128]{3,2,1,0:T(8,128)S(1)}, bf16[3,32,256]{2,1,0:T(8,128)(2,1)S(1)}, bf16[3,32,256]{2,1,0:T(8,128)(2,1)S(1)}, bf16[3,32,256]{2,1,0...) custom-call(f32[3]{0:T(128)S(1)} %copy-done.1, ...), custom_call_target="tpu_custom_call" | custom-call | tf_op jit(solution)/shard_map/pallas_call | solution.py:41
  35.0 0.1 collective-permute-start.10
  35.1 1.3 %collective-permute-start.11 = (bf16[3,32,256]{2,1,0:T(8,128)(2,1)S(1)}, bf16[3,32,256]{2,1,0:T(8,128)(2,1)S(1)}, u32[]{:S(2)}, u32[]{:S(2)}) collective-permute-start(bf16[3,32,256]{2,1,0:T(8,128)(2,1)S(1)} %get-tuple-element.74), channel_id=1, source_target_pairs={{16,32},{32,16},{48,64},{64,48},{80,96},{96,80},{112,0},{0,112},{1... | collective-permute-start | bytes 147464 | tf_op jit(solution)/shard_map/ppermute | solution.py:673
  36.4 0.5 collective-permute-start.12
  36.9 3.4 %collective-permute-start.13 = (bf16[3,32,256]{2,1,0:T(8,128)(2,1)S(1)}, bf16[3,32,256]{2,1,0:T(8,128)(2,1)S(1)}, u32[]{:S(2)}, u32[]{:S(2)}) collective-permute-start(bf16[3,32,256]{2,1,0:T(8,128)(2,1)S(1)} %get-tuple-element.76), channel_id=1, source_target_pairs={{2,4},{4,2},{6,8},{8,6},{10,12},{12,10},{14,0},{0,14},{3,5},{5,3},... | collective-permute-start | bytes 147464 | tf_op jit(solution)/shard_map/ppermute | solution.py:675
  40.3 1.5 %collective-permute-start.14 = (bf16[32,128]{1,0:T(8,128)(2,1)S(1)}, bf16[32,128]{1,0:T(8,128)(2,1)S(1)}, u32[]{:S(2)}, u32[]{:S(2)}) collective-permute-start(bf16[32,128]{1,0:T(8,128)(2,1)S(1)} %get-tuple-element.77), channel_id=1, source_target_pairs={{0,1},{1,0},{2,3},{3,2},{4,5},{5,4},{6,7},{7,6},{8,9},{9,8},{10,11... | collective-permute-start | bytes 24584 | tf_op jit(solution)/shard_map/ppermute | solution.py:676
  41.8 3.6 %collective-permute-done.14.rz = bf16[32,128]{1,0:T(8,128)(2,1)S(1)} collective-permute-done((bf16[32,128]{1,0:T(8,128)(2,1)S(1)}, bf16[32,128]{1,0:T(8,128)(2,1)S(1)}, u32[]{:S(2)}, u32[]{:S(2)}) %collective-permute-start.14) | collective-permute-done | bytes 8224 | tf_op jit(solution)/shard_map/ppermute | solution.py:676
  45.4 0.0 collective-permute-done.10.rx1
  45.4 0.0 collective-permute-done.11.rx2
  45.4 0.0 collective-permute-done.12.ry1
  45.4 0.0 collective-permute-done.13.ry2
  45.5 4.1 %shard_map.100 = (f32[3,2,1024,128]{3,2,1,0:T(8,128)S(1)}, bf16[3,32,256]{2,1,0:T(8,128)(2,1)S(1)}, bf16[3,32,256]{2,1,0:T(8,128)(2,1)S(1)}, bf16[3,32,256]{2,1,...) custom-call(f32[3]{0:T(128)S(1)} %copy-done.1, ...), custom_call_target="tpu_custom_call" | custom-call | tf_op jit(solution)/shard_map/pallas_call | solution.py:41
  49.6 0.1 collective-permute-start.15
  49.7 1.0 %collective-permute-start.16 = (bf16[3,32,256]{2,1,0:T(8,128)(2,1)S(1)}, bf16[3,32,256]{2,1,0:T(8,128)(2,1)S(1)}, u32[]{:S(2)}, u32[]{:S(2)}) collective-permute-start(bf16[3,32,256]{2,1,0:T(8,128)(2,1)S(1)} %get-tuple-element.82), channel_id=1, source_target_pairs={{16,32},{32,16},{48,64},{64,48},{80,96},{96,80},{112,0},{0,112},{1... | collective-permute-start | bytes 147464 | tf_op jit(solution)/shard_map/ppermute | solution.py:673
  50.6 0.2 collective-permute-start.17
  50.8 1.9 %collective-permute-start.18 = (bf16[3,32,256]{2,1,0:T(8,128)(2,1)S(1)}, bf16[3,32,256]{2,1,0:T(8,128)(2,1)S(1)}, u32[]{:S(2)}, u32[]{:S(2)}) collective-permute-start(bf16[3,32,256]{2,1,0:T(8,128)(2,1)S(1)} %get-tuple-element.84), channel_id=1, source_target_pairs={{2,4},{4,2},{6,8},{8,6},{10,12},{12,10},{14,0},{0,14},{3,5},{5,3},... | collective-permute-start | bytes 147464 | tf_op jit(solution)/shard_map/ppermute | solution.py:675
  52.6 1.8 %collective-permute-start.19 = (bf16[32,128]{1,0:T(8,128)(2,1)S(1)}, bf16[32,128]{1,0:T(8,128)(2,1)S(1)}, u32[]{:S(2)}, u32[]{:S(2)}) collective-permute-start(bf16[32,128]{1,0:T(8,128)(2,1)S(1)} %get-tuple-element.85), channel_id=1, source_target_pairs={{0,1},{1,0},{2,3},{3,2},{4,5},{5,4},{6,7},{7,6},{8,9},{9,8},{10,11... | collective-permute-start | bytes 24584 | tf_op jit(solution)/shard_map/ppermute | solution.py:676
  54.5 1.8 %shard_map.101 = (f32[3,32,32,256]{3,2,1,0:T(8,128)}, f32[8,128]{1,0:T(8,128)S(1)}) custom-call(f32[3,2,1024,128]{3,2,1,0:T(8,128)S(1)} %get-tuple-element.78.u), custom_call_target="tpu_custom_call" | custom-call | tf_op jit(solution)/shard_map/pallas_call | solution.py:41
  56.3 1.5 %collective-permute-done.19.rz = bf16[32,128]{1,0:T(8,128)(2,1)S(1)} collective-permute-done((bf16[32,128]{1,0:T(8,128)(2,1)S(1)}, bf16[32,128]{1,0:T(8,128)(2,1)S(1)}, u32[]{:S(2)}, u32[]{:S(2)}) %collective-permute-start.19) | collective-permute-done | bytes 8224 | tf_op jit(solution)/shard_map/ppermute | solution.py:676
  57.8 0.0 collective-permute-done.15.rx1
  57.8 0.0 collective-permute-done.16.rx2
  57.8 0.0 collective-permute-done.17.ry1
  57.8 0.0 collective-permute-done.18.ry2
  57.8 3.3 %shard_map.102 = bf16[40,32,256]{2,1,0:T(8,128)(2,1)S(1)} custom-call(f32[3,2,1024,128]{3,2,1,0:T(8,128)S(1)} %get-tuple-element.78.u, f32[2,1024,128]{2,1,0:T(8,128)S(1)} %get-tuple-element.48.tanh, f32[2,1056,128]{2,1,0:T(8,128)S(1)} %get-tuple-element.56.wx, f32[2,1024,128]{2,1,0:T(8,128)S(1)} %get-tuple-element.57.wyl, ...), custom_call_target="tpu_custom_call" | custom-call | tf_op jit(solution)/shard_map/pallas_call | solution.py:41
  61.1 0.0 copy-start.2
  61.1 0.0 copy-start.3
  61.1 13.7 %all_to_all.10.received = bf16[40,32,256]{2,1,0:T(8,128)(2,1)S(1)} all-to-all(bf16[40,32,256]{2,1,0:T(8,128)(2,1)S(1)} %shard_map.102), channel_id=1, replica_groups=mesh['gx'=8,'gy'=8,'ga'=2] {'gy'}, dimensions={0} | all-to-all | bytes 1310720 | tf_op jit(solution)/shard_map/all_to_all | solution.py:752
  74.9 0.3 shard_map.103
  75.2 11.0 %all_to_all.11.velocity = bf16[32,32,256]{2,1,0:T(8,128)(2,1)S(1)} all-to-all(bf16[32,32,256]{2,1,0:T(8,128)(2,1)S(1)} %shard_map.103), channel_id=1, replica_groups=mesh['gx'=8,'gy'=8,'ga'=2] {'gy'}, dimensions={0} | all-to-all | bytes 1048576 | tf_op jit(solution)/shard_map/all_to_all | solution.py:754
  86.2 0.0 copy-done.2
  86.2 0.0 copy-done.3
  86.2 7.0 %shard_map.104 = f32[32,32,256]{2,1,0:T(8,128)} custom-call(s32[8,16]{1,0:T(8,128)S(1)} %copy-done.2, s32[1,8]{1,0:T(1,128)S(1)} %copy-done.3, f32[2,1024,128]{2,1,0:T(8,128)S(1)} %get-tuple-element.46.lev, bf16[32,32,256]{2,1,0:T(8,128)(2,1)S(1)} %all_to_all.11.velocity, f32[2,1024,128]{2,1,0:T(8,128)S(1)} %get-tuple-element.71.held.grow, ...), custom_call_target="tpu_custom_call" | custom-call | tf_op jit(solution)/shard_map/pallas_call | solution.py:41
Async XLA Ops:
  0.6 14.8 %copy-start = (bf16[32,256]{1,0:T(8,128)(2,1)S(1)}, bf16[32,256]{1,0:T(8,128)(2,1)}, u32[]{:S(2)}) copy-start(bf16[32,256]{1,0:T(8,128)(2,1)} %extension.1) | copy-start | bytes 49156
  0.6 16.5 %copy-start.1 = (f32[3]{0:T(128)S(1)}, f32[3]{0:T(128)}, u32[]{:S(2)}) copy-start(f32[3]{0:T(128)} %traction.5) | copy-start | bytes 40
  4.0 13.1 %collective-permute-start = (bf16[4,32,256]{2,1,0:T(8,128)(2,1)S(1)}, bf16[4,32,256]{2,1,0:T(8,128)(2,1)S(1)}, u32[]{:S(2)}, u32[]{:S(2)}) collective-permute-start(bf16[4,32,256]{2,1,0:T(8,128)(2,1)S(1)} %get-tuple-element.50), channel_id=1, source_target_pairs={{0,16},{16,0},{32,48},{48,32},{64,80},{80,64},{96,112},{112,96},{1... | collective-permute-start | bytes 196616 | tf_op jit(solution)/shard_map/ppermute | solution.py:672
  4.1 13.0 %collective-permute-start.1 = (bf16[4,32,256]{2,1,0:T(8,128)(2,1)S(1)}, bf16[4,32,256]{2,1,0:T(8,128)(2,1)S(1)}, u32[]{:S(2)}, u32[]{:S(2)}) collective-permute-start(bf16[4,32,256]{2,1,0:T(8,128)(2,1)S(1)} %get-tuple-element.51), channel_id=1, source_target_pairs={{16,32},{32,16},{48,64},{64,48},{80,96},{96,80},{112,0},{0,112},{1... | collective-permute-start | bytes 196616 | tf_op jit(solution)/shard_map/ppermute | solution.py:673
  7.1 10.0 %collective-permute-start.2 = (bf16[4,32,256]{2,1,0:T(8,128)(2,1)S(1)}, bf16[4,32,256]{2,1,0:T(8,128)(2,1)S(1)}, u32[]{:S(2)}, u32[]{:S(2)}) collective-permute-start(bf16[4,32,256]{2,1,0:T(8,128)(2,1)S(1)} %get-tuple-element.52), channel_id=1, source_target_pairs={{0,2},{2,0},{4,6},{6,4},{8,10},{10,8},{12,14},{14,12},{1,3},{3,1},... | collective-permute-start | bytes 196616 | tf_op jit(solution)/shard_map/ppermute | solution.py:674
  9.0 8.1 %collective-permute-start.3 = (bf16[4,32,256]{2,1,0:T(8,128)(2,1)S(1)}, bf16[4,32,256]{2,1,0:T(8,128)(2,1)S(1)}, u32[]{:S(2)}, u32[]{:S(2)}) collective-permute-start(bf16[4,32,256]{2,1,0:T(8,128)(2,1)S(1)} %get-tuple-element.53), channel_id=1, source_target_pairs={{2,4},{4,2},{6,8},{8,6},{10,12},{12,10},{14,0},{0,14},{3,5},{5,3},... | collective-permute-start | bytes 196616 | tf_op jit(solution)/shard_map/ppermute | solution.py:675
  11.6 5.5 %collective-permute-start.4 = (bf16[32,128]{1,0:T(8,128)(2,1)S(1)}, bf16[32,128]{1,0:T(8,128)(2,1)S(1)}, u32[]{:S(2)}, u32[]{:S(2)}) collective-permute-start(bf16[32,128]{1,0:T(8,128)(2,1)S(1)} %get-tuple-element.54), channel_id=1, source_target_pairs={{0,1},{1,0},{2,3},{3,2},{4,5},{5,4},{6,7},{7,6},{8,9},{9,8},{10,11... | collective-permute-start | bytes 24584 | tf_op jit(solution)/shard_map/ppermute | solution.py:676
  22.4 8.5 %collective-permute-start.5 = (bf16[3,32,256]{2,1,0:T(8,128)(2,1)S(1)}, bf16[3,32,256]{2,1,0:T(8,128)(2,1)S(1)}, u32[]{:S(2)}, u32[]{:S(2)}) collective-permute-start(bf16[3,32,256]{2,1,0:T(8,128)(2,1)S(1)} %get-tuple-element.66), channel_id=1, source_target_pairs={{0,16},{16,0},{32,48},{48,32},{64,80},{80,64},{96,112},{112,96},{1... | collective-permute-start | bytes 147464 | tf_op jit(solution)/shard_map/ppermute | solution.py:672
  22.5 8.4 %collective-permute-start.6 = (bf16[3,32,256]{2,1,0:T(8,128)(2,1)S(1)}, bf16[3,32,256]{2,1,0:T(8,128)(2,1)S(1)}, u32[]{:S(2)}, u32[]{:S(2)}) collective-permute-start(bf16[3,32,256]{2,1,0:T(8,128)(2,1)S(1)} %get-tuple-element.67), channel_id=1, source_target_pairs={{16,32},{32,16},{48,64},{64,48},{80,96},{96,80},{112,0},{0,112},{1... | collective-permute-start | bytes 147464 | tf_op jit(solution)/shard_map/ppermute | solution.py:673
  23.4 7.5 %collective-permute-start.7 = (bf16[3,32,256]{2,1,0:T(8,128)(2,1)S(1)}, bf16[3,32,256]{2,1,0:T(8,128)(2,1)S(1)}, u32[]{:S(2)}, u32[]{:S(2)}) collective-permute-start(bf16[3,32,256]{2,1,0:T(8,128)(2,1)S(1)} %get-tuple-element.68), channel_id=1, source_target_pairs={{0,2},{2,0},{4,6},{6,4},{8,10},{10,8},{12,14},{14,12},{1,3},{3,1},... | collective-permute-start | bytes 147464 | tf_op jit(solution)/shard_map/ppermute | solution.py:674
  23.5 7.4 %collective-permute-start.8 = (bf16[3,32,256]{2,1,0:T(8,128)(2,1)S(1)}, bf16[3,32,256]{2,1,0:T(8,128)(2,1)S(1)}, u32[]{:S(2)}, u32[]{:S(2)}) collective-permute-start(bf16[3,32,256]{2,1,0:T(8,128)(2,1)S(1)} %get-tuple-element.69), channel_id=1, source_target_pairs={{2,4},{4,2},{6,8},{8,6},{10,12},{12,10},{14,0},{0,14},{3,5},{5,3},... | collective-permute-start | bytes 147464 | tf_op jit(solution)/shard_map/ppermute | solution.py:675
  25.7 5.2 %collective-permute-start.9 = (bf16[32,128]{1,0:T(8,128)(2,1)S(1)}, bf16[32,128]{1,0:T(8,128)(2,1)S(1)}, u32[]{:S(2)}, u32[]{:S(2)}) collective-permute-start(bf16[32,128]{1,0:T(8,128)(2,1)S(1)} %get-tuple-element.70), channel_id=1, source_target_pairs={{0,1},{1,0},{2,3},{3,2},{4,5},{5,4},{6,7},{7,6},{8,9},{9,8},{10,11... | collective-permute-start | bytes 24584 | tf_op jit(solution)/shard_map/ppermute | solution.py:676
  35.0 10.4 %collective-permute-start.10 = (bf16[3,32,256]{2,1,0:T(8,128)(2,1)S(1)}, bf16[3,32,256]{2,1,0:T(8,128)(2,1)S(1)}, u32[]{:S(2)}, u32[]{:S(2)}) collective-permute-start(bf16[3,32,256]{2,1,0:T(8,128)(2,1)S(1)} %get-tuple-element.73), channel_id=1, source_target_pairs={{0,16},{16,0},{32,48},{48,32},{64,80},{80,64},{96,112},{112,96},{1... | collective-permute-start | bytes 147464 | tf_op jit(solution)/shard_map/ppermute | solution.py:672
  35.1 10.3 %collective-permute-start.11 = (bf16[3,32,256]{2,1,0:T(8,128)(2,1)S(1)}, bf16[3,32,256]{2,1,0:T(8,128)(2,1)S(1)}, u32[]{:S(2)}, u32[]{:S(2)}) collective-permute-start(bf16[3,32,256]{2,1,0:T(8,128)(2,1)S(1)} %get-tuple-element.74), channel_id=1, source_target_pairs={{16,32},{32,16},{48,64},{64,48},{80,96},{96,80},{112,0},{0,112},{1... | collective-permute-start | bytes 147464 | tf_op jit(solution)/shard_map/ppermute | solution.py:673
  36.4 9.0 %collective-permute-start.12 = (bf16[3,32,256]{2,1,0:T(8,128)(2,1)S(1)}, bf16[3,32,256]{2,1,0:T(8,128)(2,1)S(1)}, u32[]{:S(2)}, u32[]{:S(2)}) collective-permute-start(bf16[3,32,256]{2,1,0:T(8,128)(2,1)S(1)} %get-tuple-element.75), channel_id=1, source_target_pairs={{0,2},{2,0},{4,6},{6,4},{8,10},{10,8},{12,14},{14,12},{1,3},{3,1},... | collective-permute-start | bytes 147464 | tf_op jit(solution)/shard_map/ppermute | solution.py:674
  36.9 8.5 %collective-permute-start.13 = (bf16[3,32,256]{2,1,0:T(8,128)(2,1)S(1)}, bf16[3,32,256]{2,1,0:T(8,128)(2,1)S(1)}, u32[]{:S(2)}, u32[]{:S(2)}) collective-permute-start(bf16[3,32,256]{2,1,0:T(8,128)(2,1)S(1)} %get-tuple-element.76), channel_id=1, source_target_pairs={{2,4},{4,2},{6,8},{8,6},{10,12},{12,10},{14,0},{0,14},{3,5},{5,3},... | collective-permute-start | bytes 147464 | tf_op jit(solution)/shard_map/ppermute | solution.py:675
  40.3 5.2 %collective-permute-start.14 = (bf16[32,128]{1,0:T(8,128)(2,1)S(1)}, bf16[32,128]{1,0:T(8,128)(2,1)S(1)}, u32[]{:S(2)}, u32[]{:S(2)}) collective-permute-start(bf16[32,128]{1,0:T(8,128)(2,1)S(1)} %get-tuple-element.77), channel_id=1, source_target_pairs={{0,1},{1,0},{2,3},{3,2},{4,5},{5,4},{6,7},{7,6},{8,9},{9,8},{10,11... | collective-permute-start | bytes 24584 | tf_op jit(solution)/shard_map/ppermute | solution.py:676
  49.6 8.2 %collective-permute-start.15 = (bf16[3,32,256]{2,1,0:T(8,128)(2,1)S(1)}, bf16[3,32,256]{2,1,0:T(8,128)(2,1)S(1)}, u32[]{:S(2)}, u32[]{:S(2)}) collective-permute-start(bf16[3,32,256]{2,1,0:T(8,128)(2,1)S(1)} %get-tuple-element.81), channel_id=1, source_target_pairs={{0,16},{16,0},{32,48},{48,32},{64,80},{80,64},{96,112},{112,96},{1... | collective-permute-start | bytes 147464 | tf_op jit(solution)/shard_map/ppermute | solution.py:672
  49.7 8.1 %collective-permute-start.16 = (bf16[3,32,256]{2,1,0:T(8,128)(2,1)S(1)}, bf16[3,32,256]{2,1,0:T(8,128)(2,1)S(1)}, u32[]{:S(2)}, u32[]{:S(2)}) collective-permute-start(bf16[3,32,256]{2,1,0:T(8,128)(2,1)S(1)} %get-tuple-element.82), channel_id=1, source_target_pairs={{16,32},{32,16},{48,64},{64,48},{80,96},{96,80},{112,0},{0,112},{1... | collective-permute-start | bytes 147464 | tf_op jit(solution)/shard_map/ppermute | solution.py:673
  50.6 7.2 %collective-permute-start.17 = (bf16[3,32,256]{2,1,0:T(8,128)(2,1)S(1)}, bf16[3,32,256]{2,1,0:T(8,128)(2,1)S(1)}, u32[]{:S(2)}, u32[]{:S(2)}) collective-permute-start(bf16[3,32,256]{2,1,0:T(8,128)(2,1)S(1)} %get-tuple-element.83), channel_id=1, source_target_pairs={{0,2},{2,0},{4,6},{6,4},{8,10},{10,8},{12,14},{14,12},{1,3},{3,1},... | collective-permute-start | bytes 147464 | tf_op jit(solution)/shard_map/ppermute | solution.py:674
  50.8 7.0 %collective-permute-start.18 = (bf16[3,32,256]{2,1,0:T(8,128)(2,1)S(1)}, bf16[3,32,256]{2,1,0:T(8,128)(2,1)S(1)}, u32[]{:S(2)}, u32[]{:S(2)}) collective-permute-start(bf16[3,32,256]{2,1,0:T(8,128)(2,1)S(1)} %get-tuple-element.84), channel_id=1, source_target_pairs={{2,4},{4,2},{6,8},{8,6},{10,12},{12,10},{14,0},{0,14},{3,5},{5,3},... | collective-permute-start | bytes 147464 | tf_op jit(solution)/shard_map/ppermute | solution.py:675
  52.6 5.2 %collective-permute-start.19 = (bf16[32,128]{1,0:T(8,128)(2,1)S(1)}, bf16[32,128]{1,0:T(8,128)(2,1)S(1)}, u32[]{:S(2)}, u32[]{:S(2)}) collective-permute-start(bf16[32,128]{1,0:T(8,128)(2,1)S(1)} %get-tuple-element.85), channel_id=1, source_target_pairs={{0,1},{1,0},{2,3},{3,2},{4,5},{5,4},{6,7},{7,6},{8,9},{9,8},{10,11... | collective-permute-start | bytes 24584 | tf_op jit(solution)/shard_map/ppermute | solution.py:676
  61.1 25.1 %copy-start.2 = (s32[8,16]{1,0:T(8,128)S(1)}, s32[8,16]{1,0:T(8,128)}, u32[]{:S(2)}) copy-start(s32[8,16]{1,0:T(8,128)} %counts.1) | copy-start | bytes 1540
  61.1 25.1 %copy-start.3 = (s32[1,8]{1,0:T(1,128)S(1)}, s32[1,8]{1,0:T(1,128)}, u32[]{:S(2)}) copy-start(s32[1,8]{1,0:T(1,128)} %listing.1) | copy-start | bytes 100
